TPU v7x, 32 devices: a whole 2x2x4 slice. The times are simulated.
32 devices in a mesh: member: 2 (over x), tile: 16 (over z, y, core).
Axes of the slice: x: 2, y: 2, z: 4, core: 2. Of those that a mesh axis runs over, the one named last changes fastest.
Arguments:
- noise_seeds: int32 [4], P('member'), parts along dimension 0, may hold values from 0 to 2147483646
- diffusivity: float32 [128, 256], P('tile'), may hold values from 0.03 to 0.24
- wet_mask: int32 [128, 256], P('tile'), may hold values 0 or 1
- vert_factor: float32 [75, 75], replicated, may hold values from -0.75 to 0.75
- norm_scale: float32 [128, 256], P('tile'), may hold values from 0.5 to 8
- obs_cell: int32 [16, 16, 128], P('tile'), may hold values from 0 to 2046, as said below
- obs_frac: float32 [16, 16, 2, 128], P('tile'), may hold values from 0 to 1
- obs_count: int32 [16, 16], P('tile'), may hold values from 32 to 128, as said below
Outputs:
- perturbation: bfloat16 [150, 128, 256], P('member', 'tile'), parts along dimension 0
- profiles: bfloat16 [16, 16, 150, 128], P('tile', None, 'member'), parts along dimension 2
There are 2 independent parts, one for each index of `member`. A program takes and returns all parts, laid end to end along the dimension named above; an argument that names none is the same for every part. Nothing has to cross between parts.
Inputs may be any that keep to these rules, and one draw needn't show every extreme that they name: `obs_cell`: each entry is row * 256 + column of an anchor cell in the owner tile's block of 8 x 256 cells, with column below 255, and row below 7 where the owner is the last tile. `obs_count`: some owner receives 128 live slots from every holder, and other counts vary by owner.
All inputs are finite; a program needn't handle non-finite values. No bound on the sum of `wet_mask` on one device may be relied on, other than what follows from the above.
Results may differ from a plain program's by a relative error of at most 0.0045.
Values may be sent and summed in bfloat16 or wider, within the bound.
No kernel may reach another device: no remote copies, remote signals or barrier semaphores. Data moves between devices by JAX's collectives and lax.ppermute only.
A program may use at most 64 MiB of HBM per device.

v0:
```python
import jax
import jax.numpy as jnp
from jax import lax
from jax.sharding import PartitionSpec as P

STEPS = 8


def extended(block, sides, width):
    for axis, dim in sides:
        count = lax.axis_size(axis)
        forward = [(i, i + 1) for i in range(count - 1)]
        backward = [(target, source) for source, target in forward]
        low = lax.ppermute(
            lax.slice_in_dim(block, block.shape[dim] - width, None, axis=dim), axis, forward
        )
        high = lax.ppermute(lax.slice_in_dim(block, 0, width, axis=dim), axis, backward)
        block = jnp.concatenate([low, block, high], axis=dim)
    return block


def from_behind(shard, axis, by):
    count = lax.axis_size(axis)
    pairs = [(i, i + by) for i in range(count) if 0 <= i + by < count]
    return lax.ppermute(shard, axis, pairs)


def scramble(hashed):
    hashed = jnp.bitwise_xor(hashed, hashed >> 16 & 65535) * -2048144789
    hashed = jnp.bitwise_xor(hashed, hashed >> 13 & 524287) * -1028477387
    return jnp.bitwise_xor(hashed, hashed >> 16 & 65535)


def cell_noise(noise_seeds, counter):
    hashed = scramble(counter * -1640531535 + noise_seeds[0])
    hashed = scramble(jnp.bitwise_xor(hashed, noise_seeds[1]))
    uniform = ((hashed >> 8 & 16777215).astype(jnp.float32) + 0.5) * (1.0 / 16777216.0)
    return (uniform - 0.5) * 3.4641016151377544


def face_terms(wet_pad):
    face_rows = jnp.sqrt(wet_pad[1:] * wet_pad[:-1])
    face_cols = jnp.sqrt(wet_pad[:, 1:] * wet_pad[:, :-1])
    return (face_rows, face_cols)


def diffuse(padded, face_rows, face_cols):
    flux_rows = face_rows[None] * (padded[:, 1:] - padded[:, :-1])
    flux_cols = face_cols[None] * (padded[:, :, 1:] - padded[:, :, :-1])
    zero_col = jnp.zeros(flux_cols.shape[:2] + (1,), jnp.float32)
    net_cols = jnp.concatenate([flux_cols, zero_col], 2) - jnp.concatenate([zero_col, flux_cols], 2)
    return padded[:, 1:-1] + (flux_rows[:, 1:] - flux_rows[:, :-1]) + net_cols[:, 1:-1]


def bilinear(flat_field, anchor, frac_y, frac_x, columns):
    corner_nw = jnp.take(flat_field, anchor, axis=1).astype(jnp.float32)
    corner_ne = jnp.take(flat_field, anchor + 1, axis=1).astype(jnp.float32)
    corner_sw = jnp.take(flat_field, anchor + columns, axis=1).astype(jnp.float32)
    corner_se = jnp.take(flat_field, anchor + columns + 1, axis=1).astype(jnp.float32)
    blended = (1.0 - frac_y) * ((1.0 - frac_x) * corner_nw + frac_x * corner_ne) + frac_y * (
        (1.0 - frac_x) * corner_sw + frac_x * corner_se
    )
    return blended


def answer_probes(flat_field, arrived, columns):
    anchor = arrived[:, 0, 0, :].astype(jnp.int32)
    blended = bilinear(flat_field, anchor, arrived[:, 0, 1, :], arrived[:, 0, 2, :], columns)
    return jnp.transpose(blended, (1, 0, 2))[:, None].astype(jnp.bfloat16)


def noise_rows(noise_seeds, levels, row_count, first_row, total_rows, columns, wet_rows):
    shape_all = (levels, row_count, columns)
    level_ids = lax.broadcasted_iota(jnp.int32, shape_all, 0)
    row_ids = lax.broadcasted_iota(jnp.int32, shape_all, 1) + first_row
    col_ids = lax.broadcasted_iota(jnp.int32, shape_all, 2)
    counter = (level_ids * total_rows + row_ids) * columns + col_ids
    return cell_noise(noise_seeds, counter) * wet_rows[None]


def sweep(padded, face_rows, face_cols, halo_depth, tile_rows):
    for inner_step in range(halo_depth):
        reach = halo_depth - inner_step
        padded = diffuse(
            padded,
            face_rows[inner_step : inner_step + tile_rows + 2 * reach - 1],
            face_cols[inner_step : inner_step + tile_rows + 2 * reach],
        )
    return padded


def body(
    noise_seeds, diffusivity, wet_mask, vert_factor, norm_scale, obs_cell, obs_frac, obs_count
):
    tile_rows, columns = diffusivity.shape
    levels = vert_factor.shape[0]
    total_rows = tile_rows * lax.axis_size("tile")
    probes = jnp.concatenate([obs_cell.astype(jnp.float32)[:, :, None, :], obs_frac], 2)
    halo_depth = STEPS
    wet_float = wet_mask.astype(jnp.float32)
    wet_kappa = diffusivity * wet_float
    wet_pad = extended(wet_kappa, (("tile", 0),), halo_depth)
    face_rows, face_cols = face_terms(wet_pad)
    first_row = lax.axis_index("tile") * tile_rows
    wet_rows = (wet_pad > 0.0).astype(jnp.float32)
    padded = noise_rows(
        noise_seeds,
        levels,
        tile_rows + 2 * halo_depth,
        first_row - halo_depth,
        total_rows,
        columns,
        wet_rows,
    )
    state_field = sweep(padded, face_rows, face_cols, halo_depth, tile_rows)
    shape_all = (levels, tile_rows, columns)
    mixed_levels = jnp.dot(
        vert_factor,
        state_field.reshape(levels, tile_rows * columns),
        precision=lax.Precision.HIGHEST,
        preferred_element_type=jnp.float32,
    )
    perturbation = (mixed_levels.reshape(shape_all) * norm_scale[None]).astype(jnp.bfloat16)
    below_row = from_behind(perturbation[:, :1], "tile", -1)
    flat_field = jnp.concatenate([perturbation, below_row], 1).reshape(
        levels, (tile_rows + 1) * columns
    )
    result = lax.all_to_all(
        answer_probes(
            flat_field,
            lax.all_to_all(probes, "tile", split_axis=1, concat_axis=0, tiled=True),
            columns,
        ),
        "tile",
        split_axis=0,
        concat_axis=1,
        tiled=True,
    )
    slot_ids = jnp.arange(result.shape[3], dtype=jnp.int32)
    live_slot = slot_ids[None, None, None, :] < obs_count[:, :, None, None]
    profiles = jnp.where(live_slot, result, jnp.zeros_like(result))
    return (perturbation, profiles)


def solution(mesh):
    in_specs = (
        P("member"),
        P("tile", None),
        P("tile", None),
        P(),
        P("tile", None),
        P("tile", None, None),
        P("tile", None, None, None),
        P("tile", None),
    )
    out_specs = (P("member", "tile", None), P("tile", None, "member", None))
    return jax.shard_map(body, mesh=mesh, in_specs=in_specs, out_specs=out_specs, check_vma=False)
```

profile of v0, /device:TPU:1, one launch (start us, length us, event | category | flops | bytes accessed | tf_op | source)
XLA Modules:
  0.0 86.9 jit_solution(14176584301633445498)
XLA Ops:
  0.6 0.7 convert_multiply_fusion
  1.4 4.5 %collective-permute-start = (f32[8,256]{1,0:T(8,128)S(1)}, f32[8,256]{1,0:T(8,128)S(1)}, u32[]{:S(2)}, u32[]{:S(2)}) collective-permute-start(f32[8,256]{1,0:T(8,128)S(1)} %convert_multiply_fusion), channel_id=1, source_target_pairs={{0,1},{1,2},{2,3},{3,4},{4,5},{5,6},{6,7},{7,8},{8,9},{9,10},{10,1... | collective-permute-start | bytes 24584 | tf_op jit(solution)/shard_map/ppermute | solution.py:14
  5.9 1.9 %collective-permute-start.1 = (f32[8,256]{1,0:T(8,128)S(1)}, f32[8,256]{1,0:T(8,128)S(1)}, u32[]{:S(2)}, u32[]{:S(2)}) collective-permute-start(f32[8,256]{1,0:T(8,128)S(1)} %convert_multiply_fusion), channel_id=1, source_target_pairs={{1,0},{2,1},{3,2},{4,3},{5,4},{6,5},{7,6},{8,7},{9,8},{10,9},{11,1... | collective-permute-start | bytes 24584 | tf_op jit(solution)/shard_map/ppermute | solution.py:17
  7.8 0.7 convert_element_type.47
  8.5 1.3 %pad_maximum_fusion.1 = f32[1,16,3,128]{3,2,0,1:T(4,128)} fusion(f32[1,16,2,128]{3,2,0,1:T(2,128)} %bitcast.75, f32[1,16,1,128]{3,2,0,1:T(1,128)S(1)} %bitcast.74), kind=kLoop, calls=%fused_computation.75 | loop fusion | flops 6144 | bytes 49152 | tf_op jit(solution)/shard_map/concatenate | solution.py:98
  9.9 6.5 %all-to-all-start = ((f32[1,16,3,128]{3,2,0,1:T(4,128)}), f32[1,16,3,128]{3,2,0,1:T(4,128)S(1)}, u32[]{:S(2)}, u32[]{:S(2)}) async-start(f32[1,16,3,128]{3,2,0,1:T(4,128)} %pad_maximum_fusion.1), calls=%async_computation | async-start | bytes 65536 | tf_op jit(solution)/shard_map/all_to_all | solution.py:131
  16.3 1.3 %fusion.37 = (s32[1]{0:T(128)}, s32[1]{0:T(128)}) fusion(s32[2]{0:T(128)} %param.10), kind=kLoop, calls=%fused_computation.102 | loop fusion | bytes 16 | tf_op jit(solution)/shard_map/slice | solution.py:35
  17.8 3.1 %add_multiply_fusion = f32[75,24,256]{2,1,0:T(8,128)S(1)} fusion(f32[24,256]{1,0:T(8,128)S(1)} %get-tuple-element.9, s32[]{:T(128)} %bitcast.1, s32[]{:T(128)} %bitcast, s32[24]{0:T(128)S(1)} %iota_add_fusion, s32[75]{0:T(128)S(1)} %iota_multiply_fusion), kind=kLoop, calls=%fused_computation.32 | loop fusion | flops 16128000 | bytes 1868180 | tf_op jit(solution)/shard_map/mul | solution.py:78
  21.3 0.5 fusion.11
  22.0 1.4 %fusion.10 = f32[75,22,256]{2,1,0:T(8,128)S(1)} fusion(f32[75,24,255]{2,1,0:T(8,128)S(1)} %fusion.11, f32[75,23,256]{2,1,0:T(8,128)S(1)} %fusion.13, f32[75,24,256]{2,1,0:T(8,128)S(1)} %add_multiply_fusion), kind=kLoop, calls=%fused_computation.25 | loop fusion | flops 1689600 | bytes 8594400 | tf_op jit(solution)/shard_map/add | solution.py:52
  23.6 0.5 fusion.7
  24.2 1.3 %fusion.6 = f32[75,20,256]{2,1,0:T(8,128)S(1)} fusion(f32[75,22,255]{2,1,0:T(8,128)S(1)} %fusion.7, f32[75,21,256]{2,1,0:T(8,128)S(1)} %fusion.9, f32[75,22,256]{2,1,0:T(8,128)S(1)} %fusion.10), kind=kLoop, calls=%fused_computation.17 | loop fusion | flops 1536000 | bytes 7827000 | tf_op jit(solution)/shard_map/add | solution.py:52
  25.8 0.5 fusion.3
  26.3 1.4 %fusion.2 = f32[75,18,256]{2,1,0:T(8,128)S(1)} fusion(f32[75,20,255]{2,1,0:T(8,128)S(1)} %fusion.3, f32[75,19,256]{2,1,0:T(8,128)S(1)} %fusion.5, f32[75,20,256]{2,1,0:T(8,128)S(1)} %fusion.6), kind=kLoop, calls=%fused_computation.9 | loop fusion | flops 1382400 | bytes 7059600 | tf_op jit(solution)/shard_map/add | solution.py:52
  28.0 0.5 fusion
  28.5 0.9 %fusion.28 = f32[75,16,256]{2,1,0:T(8,128)S(1)} fusion(f32[75,18,255]{2,1,0:T(8,128)S(1)} %fusion, f32[75,17,256]{2,1,0:T(8,128)S(1)} %fusion.1, f32[75,18,256]{2,1,0:T(8,128)S(1)} %fusion.2), kind=kLoop, calls=%fused_computation.62 | loop fusion | flops 1228800 | bytes 6292200 | tf_op jit(solution)/shard_map/add | solution.py:52
  30.0 0.8 fusion.24
  31.0 0.4 fusion.21
  31.4 0.9 %fusion.20 = f32[75,12,256]{2,1,0:T(8,128)S(1)} fusion(f32[75,14,255]{2,1,0:T(8,128)S(1)} %fusion.21, f32[75,13,256]{2,1,0:T(8,128)S(1)} %fusion.23, f32[75,14,256]{2,1,0:T(8,128)S(1)} %fusion.24), kind=kLoop, calls=%fused_computation.46 | loop fusion | flops 921600 | bytes 4757400 | tf_op jit(solution)/shard_map/add | solution.py:52
  32.9 0.7 fusion.16
  34.9 0.7 fusion.38
  36.0 2.0 %collective-permute-start.2 = (bf16[75,1,256]{2,1,0:T(2,128)(2,1)S(1)}, bf16[75,1,256]{2,1,0:T(2,128)(2,1)S(1)}, u32[]{:S(2)}, u32[]{:S(2)}) collective-permute-start(bf16[75,1,256]{2,1,0:T(2,128)(2,1)S(1)} %slice.437), channel_id=1, source_target_pairs={{1,0},{2,1},{3,2},{4,3},{5,4},{6,5},{7,6},{8,7},{9,8},{10,9},{11,1... | collective-permute-start | bytes 115208 | tf_op jit(solution)/shard_map/ppermute | solution.py:25
  38.1 3.6 %collective-permute-done.2 = bf16[75,1,256]{2,1,0:T(2,128)(2,1)S(1)} collective-permute-done((bf16[75,1,256]{2,1,0:T(2,128)(2,1)S(1)}, bf16[75,1,256]{2,1,0:T(2,128)(2,1)S(1)}, u32[]{:S(2)}, u32[]{:S(2)}) %collective-permute-start.2) | collective-permute-done | bytes 38432 | tf_op jit(solution)/shard_map/ppermute | solution.py:25
  41.8 0.5 copy.18
  42.3 6.2 %gather_fusion = bf16[2048,75]{1,0:T(8,128)(2,1)S(1)} fusion(bf16[75,2304]{0,1:T(8,128)(2,1)S(1)} %bitcast.55, s32[2048]{0:T(1024)S(1)} %get-tuple-element.14), kind=kCustom, calls=%fused_computation.clone | custom fusion | bytes 622592 | tf_op jit(solution)/shard_map/jit(_take)/gather | solution.py:56
  48.8 6.2 %gather_fusion.1 = bf16[2048,75]{1,0:T(8,128)(2,1)S(1)} fusion(bf16[75,2304]{0,1:T(8,128)(2,1)S(1)} %bitcast.56, s32[2048]{0:T(1024)S(1)} %get-tuple-element.15), kind=kCustom, calls=%fused_computation.1.clone | custom fusion | bytes 622592 | tf_op jit(solution)/shard_map/jit(_take)/gather | solution.py:57
  55.3 6.2 %gather_fusion.2 = bf16[2048,75]{1,0:T(8,128)(2,1)S(1)} fusion(bf16[75,2304]{0,1:T(8,128)(2,1)S(1)} %bitcast.57, s32[2048]{0:T(1024)S(1)} %get-tuple-element.16), kind=kCustom, calls=%fused_computation.2.clone | custom fusion | bytes 622592 | tf_op jit(solution)/shard_map/jit(_take)/gather | solution.py:58
  61.8 6.2 %gather_fusion.3 = bf16[2048,75]{1,0:T(8,128)(2,1)S(1)} fusion(bf16[75,2304]{0,1:T(8,128)(2,1)S(1)} %bitcast.58, s32[2048]{0:T(1024)S(1)} %get-tuple-element.17), kind=kCustom, calls=%fused_computation.3.clone | custom fusion | bytes 622592 | tf_op jit(solution)/shard_map/jit(_take)/gather | solution.py:59
  68.3 1.3 %fusion.33 = bf16[16,1,75,128]{3,2,1,0:T(8,128)(2,1)} fusion(bf16[16,128,75]{1,2,0:T(8,128)(2,1)S(1)} %copy.22, bf16[16,128,75]{1,2,0:T(8,128)(2,1)S(1)} %copy.21, f32[16,128]{1,0:T(8,128)S(1)} %bitcast.71, bf16[16,128,75]{1,2,0:T(8,128)(2,1)S(1)} %copy.20, f32[16,128]{1,0:T(8,128)S(1)} %bitcast.69, bf16[16,128,75]{1,2,0:T(8,128)(2,1)S(1)} %copy.19, ...), kind=kLoop, calls=%fused_computation.74 | loop fusion | flops 2764800 | bytes 1576960 | tf_op jit(solution)/shard_map/convert_element_type | solution.py:69
  69.6 5.7 %all-to-all-start.1 = ((bf16[16,1,75,128]{3,2,1,0:T(8,128)(2,1)}), bf16[16,1,75,128]{3,2,1,0:T(8,128)(2,1)S(1)}, u32[]{:S(2)}, u32[]{:S(2)}) async-start(bf16[16,1,75,128]{3,2,1,0:T(8,128)(2,1)} %fusion.33), calls=%async_computation.1 | async-start | bytes 655360 | tf_op jit(solution)/shard_map/all_to_all | solution.py:128
  75.4 10.7 %all-to-all-done.1 = bf16[16,1,75,128]{3,2,1,0:T(8,128)(2,1)S(1)} async-done(((bf16[16,1,75,128]{3,2,1,0:T(8,128)(2,1)}), bf16[16,1,75,128]{3,2,1,0:T(8,128)(2,1)S(1)}, u32[]{:S(2)}, u32[]{:S(2)}) %all-to-all-start.1) | async-done | bytes 307232 | tf_op jit(solution)/shard_map/all_to_all | solution.py:128
  86.1 0.8 copy.23
  (58 shorter events, 5.6 us)
Async XLA Ops:
  0.6 34.3 %copy-start = (f32[75,75]{1,0:T(8,128)S(1)}, f32[75,75]{1,0:T(8,128)}, u32[]{:S(2)}) copy-start(f32[75,75]{1,0:T(8,128)} %param.13) | copy-start | bytes 67504
  1.4 16.3 %collective-permute-start = (f32[8,256]{1,0:T(8,128)S(1)}, f32[8,256]{1,0:T(8,128)S(1)}, u32[]{:S(2)}, u32[]{:S(2)}) collective-permute-start(f32[8,256]{1,0:T(8,128)S(1)} %convert_multiply_fusion), channel_id=1, source_target_pairs={{0,1},{1,2},{2,3},{3,4},{4,5},{5,6},{6,7},{7,8},{8,9},{9,10},{10,1... | collective-permute-start | bytes 24584 | tf_op jit(solution)/shard_map/ppermute | solution.py:14
  5.9 11.8 %collective-permute-start.1 = (f32[8,256]{1,0:T(8,128)S(1)}, f32[8,256]{1,0:T(8,128)S(1)}, u32[]{:S(2)}, u32[]{:S(2)}) collective-permute-start(f32[8,256]{1,0:T(8,128)S(1)} %convert_multiply_fusion), channel_id=1, source_target_pairs={{1,0},{2,1},{3,2},{4,3},{5,4},{6,5},{7,6},{8,7},{9,8},{10,9},{11,1... | collective-permute-start | bytes 24584 | tf_op jit(solution)/shard_map/ppermute | solution.py:17
  9.9 28.1 %all-to-all-start = ((f32[1,16,3,128]{3,2,0,1:T(4,128)}), f32[1,16,3,128]{3,2,0,1:T(4,128)S(1)}, u32[]{:S(2)}, u32[]{:S(2)}) async-start(f32[1,16,3,128]{3,2,0,1:T(4,128)} %pad_maximum_fusion.1), calls=%async_computation | async-start | bytes 65536 | tf_op jit(solution)/shard_map/all_to_all | solution.py:131
  34.7 1.2 %copy-start.2 = (f32[8,256]{1,0:T(8,128)S(1)}, f32[8,256]{1,0:T(8,128)}, u32[]{:S(2)}) copy-start(f32[8,256]{1,0:T(8,128)} %param.14) | copy-start | bytes 24580
  35.9 12.6 %copy-start.1 = (bf16[75,8,256]{2,1,0:T(8,128)(2,1)}, bf16[75,8,256]{2,1,0:T(8,128)(2,1)S(1)}, u32[]{:S(2)}) copy-start(bf16[75,8,256]{2,1,0:T(8,128)(2,1)S(1)} %fusion.30) | copy-start | bytes 921604
  36.0 5.7 %collective-permute-start.2 = (bf16[75,1,256]{2,1,0:T(2,128)(2,1)S(1)}, bf16[75,1,256]{2,1,0:T(2,128)(2,1)S(1)}, u32[]{:S(2)}, u32[]{:S(2)}) collective-permute-start(bf16[75,1,256]{2,1,0:T(2,128)(2,1)S(1)} %slice.437), channel_id=1, source_target_pairs={{1,0},{2,1},{3,2},{4,3},{5,4},{6,5},{7,6},{8,7},{9,8},{10,9},{11,1... | collective-permute-start | bytes 115208 | tf_op jit(solution)/shard_map/ppermute | solution.py:25
  68.0 7.3 %copy-start.3 = (s32[1,16]{1,0:T(1,128)S(1)}, s32[1,16]{1,0:T(1,128)}, u32[]{:S(2)}) copy-start(s32[1,16]{1,0:T(1,128)} %param.17) | copy-start | bytes 196
  69.6 16.5 %all-to-all-start.1 = ((bf16[16,1,75,128]{3,2,1,0:T(8,128)(2,1)}), bf16[16,1,75,128]{3,2,1,0:T(8,128)(2,1)S(1)}, u32[]{:S(2)}, u32[]{:S(2)}) async-start(bf16[16,1,75,128]{3,2,1,0:T(8,128)(2,1)} %fusion.33), calls=%async_computation.1 | async-start | bytes 655360 | tf_op jit(solution)/shard_map/all_to_all | solution.py:128
where the time goes:
time: 87.8 us; the launch traced here: 86.9 us
  local copies, waits for them, and re-layouts  29.1 us (33%)
  other arithmetic  21 us (24%)
  starting transfers between devices  20.6 us (23%)
  waiting for transfers between devices  14.3 us (16%)
  between operations  1.11 us (1%)
    all_to_all x1, waiting for transfers between devices, body(): lax.all_to_all(answer_probes(flat_field, lax.all_to_all(probes, 'tile', s...  10.7 us
    add x8, other arithmetic, diffuse(): padded[:, 1:-1] + (flux_rows[:, 1:] - flux_rows[:, :-1]) + net_cols[:, 1:-1]  7.73 us
    gather x2, local copies, waits for them, and re-layouts, bilinear(): jnp.take(flat_field, anchor + columns, axis=1).astype(jnp.float32)  6.47 us
    gather x2, local copies, waits for them, and re-layouts, bilinear(): corner_ne = jnp.take(flat_field, anchor + 1, axis=1).astype(jnp.float32)  6.47 us
    gather x2, local copies, waits for them, and re-layouts, bilinear(): jnp.take(flat_field, anchor + columns + 1, axis=1).astype(jnp.float32)  6.47 us
    gather x2, local copies, waits for them, and re-layouts, bilinear(): corner_nw = jnp.take(flat_field, anchor, axis=1).astype(jnp.float32)  6.47 us
    all_to_all x1, starting transfers between devices, body(): lax.all_to_all(probes, 'tile', split_axis=1, concat_axis=0, tiled=True)  6.45 us
    all_to_all x1, starting transfers between devices, body(): lax.all_to_all(answer_probes(flat_field, lax.all_to_all(probes, 'tile', s...  5.73 us
  transfers between devices with their start and end apart: 5, of which 2 were waited for; matrix products, arithmetic and copies ran while one was open for 25% of the time, Pallas kernels for 0%

commit v1 on v0

v1 whole, which is shorter than its diff:
```python
import jax
import jax.numpy as jnp
from jax import lax
from jax.experimental import pallas as pl
from jax.experimental.pallas import tpu as pltpu
from jax.sharding import PartitionSpec as P

STEPS = 8
LANES = 128
SUB = 8
EXACT = lax.Precision.HIGHEST
F32 = jnp.float32
I32 = jnp.int32
GOLDEN = -1640531535
ROOT12 = 3.4641016151377544
VMEM = pl.BlockSpec(memory_space=pltpu.VMEM)
SMEM = pl.BlockSpec(memory_space=pltpu.SMEM)


def up(value, unit):
    return -(-value // unit) * unit


def wrapped(value):
    return (value + 2**31) % 2**32 - 2**31


def iota(shape, axis):
    return lax.broadcasted_iota(I32, shape, axis)


def split_columns(columns):
    half = columns // 2
    col = iota((columns, columns), 0)
    place = iota((columns, columns), 1)
    source = jnp.where(place < half, 2 * place, 2 * (place - half) + 1)
    return col == source


def pack_kernel(diff_ref, wet_ref, norm_ref, cell_ref, frac_ref, count_ref, out_ref, norm_out):
    tile_rows, columns = diff_ref.shape
    half = columns // 2
    owners = cell_ref.shape[0]
    kappa = diff_ref[...] * wet_ref[...].astype(F32)
    both = jnp.concatenate([kappa, norm_ref[...]], 0)
    parted = jnp.dot(
        both, split_columns(columns).astype(F32), precision=EXACT, preferred_element_type=F32
    )
    kappa_even, kappa_odd = parted[:tile_rows, :half], parted[:tile_rows, half:]
    norm_even, norm_odd = parted[tile_rows:, :half], parted[tile_rows:, half:]
    norm_out[:tile_rows] = norm_even
    norm_out[tile_rows:] = norm_odd
    cell = cell_ref[...]
    row = jnp.zeros_like(cell)
    for step in range(1, tile_rows):
        row = row + (cell >= step * columns).astype(I32)
    col = cell - row * columns
    pos_y = row.astype(F32) + frac_ref[:, 0, :]
    pos_x = col.astype(F32) + frac_ref[:, 1, :]
    lane = iota((1, LANES), 1)
    for owner in range(owners):
        out_ref[owner, :tile_rows, :] = kappa_even
        out_ref[owner, tile_rows : 2 * tile_rows, :] = kappa_odd
        live = lane < count_ref[0, owner]
        tail = jnp.concatenate(
            [
                norm_even[:1],
                norm_odd[:1],
                pos_x[owner : owner + 1],
                jnp.where(live, pos_y[owner : owner + 1], -2.0),
                jnp.zeros((SUB - 4, LANES), F32),
            ],
            0,
        )
        out_ref[owner, 2 * tile_rows :, :] = tail


def mix(hashed, second):
    hashed = (hashed ^ lax.shift_right_logical(hashed, 16)) * -2048144789
    hashed = (hashed ^ lax.shift_right_logical(hashed, 13)) * -1028477387
    hashed = hashed ^ lax.shift_right_logical(hashed, 16)
    return hashed


def noise_kernel(total_rows, tile_rows, columns, seed_ref, out_ref):
    planes, levels, _ = out_ref.shape
    first_row = lax.axis_index("tile") * tile_rows - STEPS
    step_level = wrapped(total_rows * columns * GOLDEN)
    shape = (SUB, LANES)
    base = iota(shape, 0) * step_level + iota(shape, 1) * wrapped(2 * GOLDEN)
    gain = ROOT12 / 16777216.0
    shift = (0.5 / 16777216.0 - 0.5) * ROOT12
    origin = first_row * wrapped(columns * GOLDEN) + seed_ref[0]
    second = seed_ref[1]

    def one_tile(block, carry):
        start = origin + block * wrapped(SUB * step_level)
        for plane in range(planes):
            offset = start + wrapped(((plane // 2) * columns + plane % 2) * GOLDEN)
            hashed = mix(mix(base + offset, None) ^ second, None)
            level = pl.multiple_of(block * SUB, SUB)
            drawn = lax.shift_right_logical(hashed, 8).astype(F32)
            out_ref[plane, pl.ds(level, SUB), :] = drawn * gain + shift
        return carry

    lax.fori_loop(0, levels // SUB, one_tile, 0)


def field_kernel(
    tiles, noise_ref, recv_ref, norm_ref, vert_ref, prof_ref, field_ref,
    even_ref, odd_ref, root_ref, keep_ref, gain_ref, vert_pad, state_ref,
):
    planes, levels, half = noise_ref.shape
    rows = planes // 2
    columns = 2 * half
    tile_rows = norm_ref.shape[0] // 2
    depth = vert_ref.shape[0]
    out_rows = tile_rows + 1
    tile = lax.axis_index("tile")

    even_ref[...] = jnp.zeros_like(even_ref)
    odd_ref[...] = jnp.zeros_like(odd_ref)
    for place, (shift, count) in enumerate(((-1, tile_rows), (0, tile_rows), (1, tile_rows), (2, 1))):
        source = tile + shift
        valid = ((source >= 0) & (source < tiles)).astype(F32)
        source = jnp.clip(source, 0, tiles - 1)
        start = place * tile_rows
        even_ref[start : start + count] = recv_ref[source, :count, :] * valid
        odd_ref[start : start + count] = recv_ref[source, tile_rows : tile_rows + count, :] * valid
    kappa_even, kappa_odd = even_ref[...], odd_ref[...]
    below = jnp.clip(tile + 1, 0, tiles - 1)
    even_ref[...] = jnp.sqrt(kappa_even)
    odd_ref[...] = jnp.sqrt(kappa_odd)
    root_even, root_odd = even_ref[...], odd_ref[...]
    lane = iota((1, LANES), 1)
    first, last = lane == 0, lane == LANES - 1
    inner = slice(1, rows - 1)
    for parity, (mine, other, mine_ref, edge, turn) in enumerate((
        (root_even, root_odd, even_ref, first, 1),
        (root_odd, root_even, odd_ref, last, LANES - 1),
    )):
        turned = jnp.where(edge, 0.0, pltpu.roll(other, turn, 1))
        near = mine_ref[: rows - 2] + mine_ref[2:rows] + (other + turned)[inner]
        keep = 1.0 - mine[inner] * near
        gain = mine[inner] * mine[inner]
        for row in range(rows):
            spread = (SUB, LANES)
            root_ref[2 * row + parity] = jnp.broadcast_to(mine[row : row + 1], spread)
            if 0 < row < rows - 1:
                keep_ref[2 * row + parity] = jnp.broadcast_to(keep[row - 1 : row], spread)
                gain_ref[2 * row + parity] = jnp.broadcast_to(gain[row - 1 : row], spread)
    own = slice(STEPS, STEPS + out_rows)
    scales = []
    for parity, (root, kappa) in enumerate(((root_even, kappa_even), (root_odd, kappa_odd))):
        wet = kappa[own] > 0.0
        inverse = jnp.where(wet, root[own] / jnp.where(wet, kappa[own], 1.0), 0.0)
        norm = jnp.concatenate(
            [
                norm_ref[parity * tile_rows : (parity + 1) * tile_rows],
                recv_ref[below, 2 * tile_rows + parity : 2 * tile_rows + parity + 1, :],
            ],
            0,
        )
        scales.append(inverse * norm)

    block = (SUB, LANES)
    first8, last8 = iota(block, 1) == 0, iota(block, 1) == LANES - 1

    def diffuse(part, carry):
        span = pl.ds(pl.multiple_of(part * SUB, SUB), SUB)
        even = [noise_ref[2 * row, span, :] * root_ref[2 * row] for row in range(rows)]
        odd = [noise_ref[2 * row + 1, span, :] * root_ref[2 * row + 1] for row in range(rows)]
        for step in range(STEPS):
            next_even, next_odd = [], []
            for j in range(1, len(even) - 1):
                at = 2 * (j + step)
                e, o = even[j], odd[j]
                west = jnp.where(first8, 0.0, pltpu.roll(o, 1, 1))
                east = jnp.where(last8, 0.0, pltpu.roll(e, LANES - 1, 1))
                sum_e = (even[j - 1] + even[j + 1]) + (o + west)
                sum_o = (odd[j - 1] + odd[j + 1]) + (e + east)
                next_even.append(keep_ref[at] * e + gain_ref[at] * sum_e)
                next_odd.append(keep_ref[at + 1] * o + gain_ref[at + 1] * sum_o)
            even, odd = next_even, next_odd
        for row in range(out_rows):
            state_ref[span, row * columns : row * columns + half] = even[row]
            state_ref[span, row * columns + half : (row + 1) * columns] = odd[row]
        return carry

    lax.fori_loop(0, levels // SUB, diffuse, 0)

    vert_pad[...] = jnp.zeros_like(vert_pad)
    vert_pad[:depth, :depth] = vert_ref[...]
    factor = vert_pad[...]
    for row in range(out_rows):
        scale = jnp.concatenate([scales[0][row : row + 1], scales[1][row : row + 1]], 1)
        mixed = jnp.dot(
            factor,
            state_ref[:, row * columns : (row + 1) * columns],
            precision=EXACT,
            preferred_element_type=F32,
        )
        field_ref[row * levels : (row + 1) * levels, :] = (mixed * scale).astype(jnp.bfloat16)

    place = iota((columns, 2 * LANES), 0)
    col = jnp.where(place < half, 2 * place, 2 * (place - half) + 1).astype(F32)

    def interpolate(pair, carry):
        tails = [recv_ref[2 * pair + k, 2 * tile_rows :, :] for k in range(2)]
        pos_x = jnp.concatenate([tails[0][2:3], tails[1][2:3]], 1)
        pos_y = jnp.concatenate([tails[0][3:4], tails[1][3:4]], 1)
        hat = jnp.maximum(1.0 - jnp.abs(pos_x - col), 0.0).astype(jnp.bfloat16)
        total = None
        for row in range(out_rows):
            along = jnp.dot(
                field_ref[row * levels : (row + 1) * levels, :], hat, preferred_element_type=F32
            )
            weight = jnp.maximum(1.0 - jnp.abs(pos_y - float(row)), 0.0)
            total = along * weight if total is None else total + along * weight
        rounded = total[:depth].astype(jnp.bfloat16)
        prof_ref[2 * pair] = rounded[:, :LANES]
        prof_ref[2 * pair + 1] = rounded[:, LANES:]
        return carry

    lax.fori_loop(0, tiles // 2, interpolate, 0)


def weave_kernel(field_ref, out_ref, flat_ref):
    depth, tile_rows, columns = out_ref.shape
    levels = field_ref.shape[0] // (tile_rows + 1)
    half = columns // 2
    place = iota((columns, columns), 0)
    col = iota((columns, columns), 1)
    source = jnp.where(place < half, 2 * place, 2 * (place - half) + 1)
    weave = (col == source).astype(jnp.bfloat16)
    for row in range(tile_rows):
        woven = jnp.dot(
            field_ref[row * levels : (row + 1) * levels, :], weave, preferred_element_type=F32
        )
        flat_ref[:, row, :] = woven
    out_ref[...] = flat_ref[:depth].astype(jnp.bfloat16)


def body(
    noise_seeds, diffusivity, wet_mask, vert_factor, norm_scale, obs_cell, obs_frac, obs_count
):
    tile_rows, columns = diffusivity.shape
    depth = vert_factor.shape[0]
    levels = up(depth, 2 * SUB)
    tiles = lax.axis_size("tile")
    total_rows = tile_rows * tiles
    half = columns // 2
    rows = tile_rows + 1 + 2 * STEPS
    slots = obs_cell.shape[2]

    packed, norm_split = pl.pallas_call(
        pack_kernel,
        out_shape=(
            jax.ShapeDtypeStruct((tiles, 2 * tile_rows + SUB, LANES), F32),
            jax.ShapeDtypeStruct((2 * tile_rows, half), F32),
        ),
        in_specs=[VMEM] * 5 + [SMEM],
        out_specs=(VMEM, VMEM),
        name="pack",
    )(diffusivity, wet_mask, norm_scale, obs_cell[0], obs_frac[0], obs_count)
    received = lax.all_to_all(packed, "tile", split_axis=0, concat_axis=0, tiled=True)

    noise = pl.pallas_call(
        lambda *refs: noise_kernel(total_rows, tile_rows, columns, *refs),
        out_shape=jax.ShapeDtypeStruct((2 * rows, levels, half), F32),
        in_specs=[SMEM],
        out_specs=VMEM,
        name="noise",
    )(noise_seeds)

    flat = (2 * rows, SUB, LANES)
    answers, field = pl.pallas_call(
        lambda *refs: field_kernel(tiles, *refs),
        out_shape=(
            jax.ShapeDtypeStruct((tiles, depth, slots), jnp.bfloat16),
            jax.ShapeDtypeStruct(((tile_rows + 1) * levels, columns), jnp.bfloat16),
        ),
        in_specs=[VMEM] * 4,
        out_specs=(VMEM, VMEM),
        scratch_shapes=[
            pltpu.VMEM((up(rows, SUB), half), F32),
            pltpu.VMEM((up(rows, SUB), half), F32),
            pltpu.VMEM(flat, F32),
            pltpu.VMEM(flat, F32),
            pltpu.VMEM(flat, F32),
            pltpu.VMEM((levels, levels), F32),
            pltpu.VMEM((levels, (tile_rows + 1) * columns), F32),
        ],
        name="field",
    )(noise, received, norm_split, vert_factor)
    profiles = lax.all_to_all(answers, "tile", split_axis=0, concat_axis=0, tiled=True)

    perturbation = pl.pallas_call(
        weave_kernel,
        out_shape=jax.ShapeDtypeStruct((depth, tile_rows, columns), jnp.bfloat16),
        in_specs=[VMEM],
        out_specs=VMEM,
        scratch_shapes=[pltpu.VMEM((levels, tile_rows, columns), F32)],
        name="weave",
    )(field)
    return (perturbation, profiles[None])


def solution(mesh):
    in_specs = (
        P("member"),
        P("tile", None),
        P("tile", None),
        P(),
        P("tile", None),
        P("tile", None, None),
        P("tile", None, None, None),
        P("tile", None),
    )
    out_specs = (P("member", "tile", None), P("tile", None, "member", None))
    return jax.shard_map(body, mesh=mesh, in_specs=in_specs, out_specs=out_specs, check_vma=False)
```

time: 87.8 us -> 47.6 us (0.54)
  local copies, waits for them, and re-layouts: 29.1 us -> 1.47 us
  other arithmetic: 21 us -> 0 us
  Pallas kernels: 0 us -> 19.9 us
  starting transfers between devices: 20.6 us -> 11.4 us
  waiting for transfers between devices: 14.3 us -> 13.3 us
    gather x8 -> x0, local copies, waits for them, and re-layouts: 25.9 us -> none  [the longest x2 6.47 us: bilinear(): jnp.take(flat_field, anchor + columns, axis=1).astype(jnp.float32)]
    pallas_call x0 -> x4, Pallas kernels: none -> 19.9 us  [the longest x1 12.4 us: body(): pl.pallas_call(lambda *refs: field_kernel(tiles, *refs), out_shape=(jax.S...]
    mul x19 -> x0, other arithmetic: 9.52 us -> none  [the longest x8 3.72 us: diffuse(): flux_cols = face_cols[None] * (padded[:, :, 1:] - padded[:, :, :-1])]
    ppermute x3 -> x0, starting transfers between devices: 8.45 us -> none  [the longest x1 4.51 us: extended(): lax.ppermute(lax.slice_in_dim(block, block.shape[dim] - width, None, axis...]
    add x9 -> x0, other arithmetic: 7.73 us -> none  [the longest x8 7.73 us: diffuse(): padded[:, 1:-1] + (flux_rows[:, 1:] - flux_rows[:, :-1]) + net_cols[:, 1:-1]]
    ppermute x3 -> x0, waiting for transfers between devices: 3.59 us -> none  [the longest x1 3.58 us: from_behind(): return lax.ppermute(shard, axis, pairs)]
    all_to_all x2, waiting for transfers between devices: 10.7 us -> 13.3 us  [the longest x1 8.74 us: body(): lax.all_to_all(answers, 'tile', split_axis=0, concat_axis=0, tiled=True)]
    convert_element_type x3 -> x0, other arithmetic: 2.07 us -> none  [the longest x1 1.31 us: answer_probes(): return jnp.transpose(blended, (1, 0, 2))[:, None].astype(jnp.bfloat16)]
  transfers between devices with their start and end apart: 5 -> 2, of which waited for: 2 -> 2; matrix products, arithmetic and copies ran while one was open for 25% -> 0% of each run, Pallas kernels for 0% -> 12%
where the time goes in v1:
time: 47.6 us; the launch traced here: 46.8 us
  Pallas kernels  19.9 us (42%)
  waiting for transfers between devices  13.3 us (28%)
  starting transfers between devices  11.4 us (24%)
  local copies, waits for them, and re-layouts  1.47 us (3%)
  between operations  0.64 us (1%)
    pallas_call x1, Pallas kernels, body(): pl.pallas_call(lambda *refs: field_kernel(tiles, *refs), out_shape=(jax.S...  12.4 us
    all_to_all x1, waiting for transfers between devices, body(): lax.all_to_all(answers, 'tile', split_axis=0, concat_axis=0, tiled=True)  8.74 us
    all_to_all x1, starting transfers between devices, body(): lax.all_to_all(packed, 'tile', split_axis=0, concat_axis=0, tiled=True)  7.34 us
    all_to_all x1, waiting for transfers between devices, body(): lax.all_to_all(packed, 'tile', split_axis=0, concat_axis=0, tiled=True)  4.6 us
    all_to_all x1, starting transfers between devices, body(): lax.all_to_all(answers, 'tile', split_axis=0, concat_axis=0, tiled=True)  4.1 us
    pallas_call x1, Pallas kernels, body(): pl.pallas_call(lambda *refs: noise_kernel(total_rows, tile_rows, columns,...  3.68 us
    pallas_call x1, Pallas kernels, body(): pl.pallas_call(weave_kernel, out_shape=jax.ShapeDtypeStruct((depth, tile_...  2.12 us
    pallas_call x1, Pallas kernels, body(): pl.pallas_call(pack_kernel, out_shape=(jax.ShapeDtypeStruct((tiles, 2 * t...  1.73 us
  transfers between devices with their start and end apart: 2, of which 2 were waited for; matrix products, arithmetic and copies ran while one was open for 0% of the time, Pallas kernels for 12%

profile of v1, /device:TPU:1, one launch (start us, length us, event | category | flops | bytes accessed | tf_op | source)
XLA Modules:
  0.0 46.8 jit_solution(11300793199503881365)
XLA Ops:
  0.6 1.7 %pack.1 = (f32[16,24,128]{2,1,0:T(8,128)}, f32[16,128]{1,0:T(8,128)}) custom-call(f32[8,256]{1,0:T(8,128)} %diff_ref.1, s32[8,256]{1,0:T(8,128)} %wet_ref.1, f32[8,256]{1,0:T(8,128)} %norm_ref.1, s32[16,128]{1,0:T(8,128)} %bitcast.5, f32[16,2,128]{2,1,0:T(2,128)} %bitcast.4, s32[1,16]{1,0:T(1,128)} %count_ref.1), custom_call_target="tpu_custom_call" | custom-call | tf_op jit(solution)/shard_map/pack/pallas_call | solution.py:256
  2.4 7.3 %all-to-all-start = ((f32[16,24,128]{2,1,0:T(8,128)}), f32[16,24,128]{2,1,0:T(8,128)S(1)}, u32[]{:S(2)}, u32[]{:S(2)}) async-start(f32[16,24,128]{2,1,0:T(8,128)} %get-tuple-element.6), calls=%async_computation | async-start | bytes 393216 | tf_op jit(solution)/shard_map/all_to_all | solution.py:266
  9.7 3.7 %noise.1.refs_0_ = f32[50,80,128]{2,1,0:T(8,128)} custom-call(s32[2]{0:T(128)} %refs_0_.1), custom_call_target="tpu_custom_call" | custom-call | tf_op jit(solution)/shard_map/noise/pallas_call | solution.py:268
  13.4 4.6 %all-to-all-done.refs_1_ = f32[16,24,128]{2,1,0:T(8,128)S(1)} async-done(((f32[16,24,128]{2,1,0:T(8,128)}), f32[16,24,128]{2,1,0:T(8,128)S(1)}, u32[]{:S(2)}, u32[]{:S(2)}) %all-to-all-start) | async-done | bytes 196640 | tf_op jit(solution)/shard_map/all_to_all | solution.py:266
  18.0 0.0 copy-start
  18.0 0.7 %copy-done = f32[16,24,128]{2,1,0:T(8,128)} copy-done((f32[16,24,128]{2,1,0:T(8,128)}, f32[16,24,128]{2,1,0:T(8,128)S(1)}, u32[]{:S(2)}) %copy-start) | copy-done | bytes 196632
  18.7 12.4 %field.1 = (bf16[16,75,128]{2,1,0:T(8,128)(2,1)}, bf16[720,256]{1,0:T(8,128)(2,1)}) custom-call(f32[50,80,128]{2,1,0:T(8,128)} %noise.1.refs_0_, f32[16,24,128]{2,1,0:T(8,128)} %copy-done, f32[16,128]{1,0:T(8,128)} %get-tuple-element.7.refs_2_, f32[75,75]{1,0:T(8,128)} %refs_3_.1), custom_call_target="tpu_custom_call" | custom-call | tf_op jit(solution)/shard_map/field/pallas_call | solution.py:277
  31.1 4.1 %all-to-all-start.1 = ((bf16[16,75,128]{2,1,0:T(8,128)(2,1)}), bf16[16,75,128]{2,1,0:T(8,128)(2,1)S(1)}, u32[]{:S(2)}, u32[]{:S(2)}) async-start(bf16[16,75,128]{2,1,0:T(8,128)(2,1)} %get-tuple-element.9), calls=%async_computation.1 | async-start | bytes 655360 | tf_op jit(solution)/shard_map/all_to_all | solution.py:296
  35.2 2.1 %weave.1 = bf16[75,8,256]{2,1,0:T(8,128)(2,1)} custom-call(bf16[720,256]{1,0:T(8,128)(2,1)} %get-tuple-element.8.field_ref), custom_call_target="tpu_custom_call" | custom-call | tf_op jit(solution)/shard_map/weave/pallas_call | solution.py:298
  37.3 8.7 %all-to-all-done.1 = bf16[16,75,128]{2,1,0:T(8,128)(2,1)S(1)} async-done(((bf16[16,75,128]{2,1,0:T(8,128)(2,1)}), bf16[16,75,128]{2,1,0:T(8,128)(2,1)S(1)}, u32[]{:S(2)}, u32[]{:S(2)}) %all-to-all-start.1) | async-done | bytes 307232 | tf_op jit(solution)/shard_map/all_to_all | solution.py:296
  46.0 0.8 %copy.10 = bf16[1,16,75,128]{3,1,2,0:T(8,128)(2,1)} copy(bf16[1,16,75,128]{3,2,1,0:T(8,128)(2,1)S(1)} %bitcast.3) | data formatting | bytes 614400
Async XLA Ops:
  2.4 15.6 %all-to-all-start = ((f32[16,24,128]{2,1,0:T(8,128)}), f32[16,24,128]{2,1,0:T(8,128)S(1)}, u32[]{:S(2)}, u32[]{:S(2)}) async-start(f32[16,24,128]{2,1,0:T(8,128)} %get-tuple-element.6), calls=%async_computation | async-start | bytes 393216 | tf_op jit(solution)/shard_map/all_to_all | solution.py:266
  18.0 0.7 %copy-start = (f32[16,24,128]{2,1,0:T(8,128)}, f32[16,24,128]{2,1,0:T(8,128)S(1)}, u32[]{:S(2)}) copy-start(f32[16,24,128]{2,1,0:T(8,128)S(1)} %all-to-all-done.refs_1_) | copy-start | bytes 589828
  31.1 15.0 %all-to-all-start.1 = ((bf16[16,75,128]{2,1,0:T(8,128)(2,1)}), bf16[16,75,128]{2,1,0:T(8,128)(2,1)S(1)}, u32[]{:S(2)}, u32[]{:S(2)}) async-start(bf16[16,75,128]{2,1,0:T(8,128)(2,1)} %get-tuple-element.9), calls=%async_computation.1 | async-start | bytes 655360 | tf_op jit(solution)/shard_map/all_to_all | solution.py:296

commit v2 on v1

--- a/solution.py
+++ b/solution.py
@@ -15,6 +15,11 @@
 ROOT12 = 3.4641016151377544
 VMEM = pl.BlockSpec(memory_space=pltpu.VMEM)
 SMEM = pl.BlockSpec(memory_space=pltpu.SMEM)
+LIMIT = pltpu.CompilerParams(vmem_limit_bytes=24 << 20)
+
+
+def resident(array):
+    return pltpu.with_memory_space_constraint(array, pltpu.VMEM)
 
 
 def up(value, unit):
@@ -267,10 +272,11 @@
 
     noise = pl.pallas_call(
         lambda *refs: noise_kernel(total_rows, tile_rows, columns, *refs),
-        out_shape=jax.ShapeDtypeStruct((2 * rows, levels, half), F32),
+        out_shape=pltpu.VMEM((2 * rows, levels, half), F32),
         in_specs=[SMEM],
         out_specs=VMEM,
         name="noise",
+        compiler_params=LIMIT,
     )(noise_seeds)
 
     flat = (2 * rows, SUB, LANES)
@@ -278,7 +284,7 @@
         lambda *refs: field_kernel(tiles, *refs),
         out_shape=(
             jax.ShapeDtypeStruct((tiles, depth, slots), jnp.bfloat16),
-            jax.ShapeDtypeStruct(((tile_rows + 1) * levels, columns), jnp.bfloat16),
+            pltpu.VMEM(((tile_rows + 1) * levels, columns), jnp.bfloat16),
         ),
         in_specs=[VMEM] * 4,
         out_specs=(VMEM, VMEM),
@@ -292,7 +298,8 @@
             pltpu.VMEM((levels, (tile_rows + 1) * columns), F32),
         ],
         name="field",
-    )(noise, received, norm_split, vert_factor)
+        compiler_params=LIMIT,
+    )(resident(noise), resident(received), resident(norm_split), vert_factor)
     profiles = lax.all_to_all(answers, "tile", split_axis=0, concat_axis=0, tiled=True)
 
     perturbation = pl.pallas_call(
@@ -302,7 +309,8 @@
         out_specs=VMEM,
         scratch_shapes=[pltpu.VMEM((levels, tile_rows, columns), F32)],
         name="weave",
-    )(field)
+        compiler_params=LIMIT,
+    )(resident(field))
     return (perturbation, profiles[None])
 
 

time: 47.6 us -> 45.4 us (0.954)
  Pallas kernels: 19.9 us -> 15.8 us
  waiting for transfers between devices: 13.3 us -> 15.1 us
    pallas_call x1, Pallas kernels: 12.4 us -> 10.7 us  [body(): pl.pallas_call(lambda *refs: field_kernel(tiles, *refs), out_shape=(jax.S...]
    pallas_call x1, Pallas kernels: 3.68 us -> 2.24 us  [body(): pl.pallas_call(lambda *refs: noise_kernel(total_rows, tile_rows, columns,...]
    pallas_call x1, Pallas kernels: 2.12 us -> 1.13 us  [body(): pl.pallas_call(weave_kernel, out_shape=jax.ShapeDtypeStruct((depth, tile_...]
    all_to_all x1, waiting for transfers between devices: 8.74 us -> 9.72 us  [body(): lax.all_to_all(answers, 'tile', split_axis=0, concat_axis=0, tiled=True)]
    all_to_all x1, waiting for transfers between devices: 4.6 us -> 5.38 us  [body(): lax.all_to_all(packed, 'tile', split_axis=0, concat_axis=0, tiled=True)]
    unnamed x3 -> x7, local copies, waits for them, and re-layouts: 1.47 us -> 1.45 us
  transfers between devices with their start and end apart: 2 -> 2, of which waited for: 2 -> 2; matrix products, arithmetic and copies ran while one was open for 0% -> 0% of each run, Pallas kernels for 12% -> 8%
where the time goes in v2:
time: 45.4 us; the launch traced here: 44.6 us
  Pallas kernels  15.8 us (35%)
  waiting for transfers between devices  15.1 us (33%)
  starting transfers between devices  11.6 us (26%)
  local copies, waits for them, and re-layouts  1.45 us (3%)
  between operations  0.66 us (1%)
    pallas_call x1, Pallas kernels, body(): pl.pallas_call(lambda *refs: field_kernel(tiles, *refs), out_shape=(jax.S...  10.7 us
    all_to_all x1, waiting for transfers between devices, body(): lax.all_to_all(answers, 'tile', split_axis=0, concat_axis=0, tiled=True)  9.72 us
    all_to_all x1, starting transfers between devices, body(): lax.all_to_all(packed, 'tile', split_axis=0, concat_axis=0, tiled=True)  7.47 us
    all_to_all x1, waiting for transfers between devices, body(): lax.all_to_all(packed, 'tile', split_axis=0, concat_axis=0, tiled=True)  5.38 us
    all_to_all x1, starting transfers between devices, body(): lax.all_to_all(answers, 'tile', split_axis=0, concat_axis=0, tiled=True)  4.1 us
    pallas_call x1, Pallas kernels, body(): pl.pallas_call(lambda *refs: noise_kernel(total_rows, tile_rows, columns,...  2.24 us
    pallas_call x1, Pallas kernels, body(): pl.pallas_call(pack_kernel, out_shape=(jax.ShapeDtypeStruct((tiles, 2 * t...  1.73 us
    unnamed x7, local copies, waits for them, and re-layouts  1.45 us
  transfers between devices with their start and end apart: 2, of which 2 were waited for; matrix products, arithmetic and copies ran while one was open for 0% of the time, Pallas kernels for 8%

profile of v2, /device:TPU:1, one launch (start us, length us, event | category | flops | bytes accessed | tf_op | source)
XLA Modules:
  0.0 44.6 jit_solution(12440663994478340721)
XLA Ops:
  0.6 0.0 copy-start
  0.6 1.7 %pack.1 = (f32[16,24,128]{2,1,0:T(8,128)}, f32[16,128]{1,0:T(8,128)}) custom-call(f32[8,256]{1,0:T(8,128)} %diff_ref.1, s32[8,256]{1,0:T(8,128)} %wet_ref.1, f32[8,256]{1,0:T(8,128)} %norm_ref.1, s32[16,128]{1,0:T(8,128)} %bitcast.5, f32[16,2,128]{2,1,0:T(2,128)} %bitcast.4, s32[1,16]{1,0:T(1,128)} %count_ref.1), custom_call_target="tpu_custom_call" | custom-call | tf_op jit(solution)/shard_map/pack/pallas_call | solution.py:261
  2.4 0.0 copy-start.1
  2.4 7.5 %all-to-all-start = ((f32[16,24,128]{2,1,0:T(8,128)}), f32[16,24,128]{2,1,0:T(8,128)S(1)}, u32[]{:S(2)}, u32[]{:S(2)}) async-start(f32[16,24,128]{2,1,0:T(8,128)} %get-tuple-element.6), calls=%async_computation | async-start | bytes 393216 | tf_op jit(solution)/shard_map/all_to_all | solution.py:271
  9.8 0.0 copy-start.2
  9.9 0.6 %copy-done.2 = s32[2]{0:T(128)S(1)} copy-done((s32[2]{0:T(128)S(1)}, s32[2]{0:T(128)}, u32[]{:S(2)}) %copy-start.2) | copy-done | bytes 32
  10.5 2.2 %noise.1.refs_0_ = f32[50,80,128]{2,1,0:T(8,128)S(1)} custom-call(s32[2]{0:T(128)S(1)} %copy-done.2), custom_call_target="tpu_custom_call" | custom-call | tf_op jit(solution)/shard_map/noise/pallas_call | solution.py:273
  12.8 5.4 %all-to-all-done.refs_1_ = f32[16,24,128]{2,1,0:T(8,128)S(1)} async-done(((f32[16,24,128]{2,1,0:T(8,128)}), f32[16,24,128]{2,1,0:T(8,128)S(1)}, u32[]{:S(2)}, u32[]{:S(2)}) %all-to-all-start) | async-done | bytes 196640 | tf_op jit(solution)/shard_map/all_to_all | solution.py:271
  18.1 0.0 copy-done
  18.1 0.0 copy-done.1
  18.1 10.7 %field.1 = (bf16[16,75,128]{2,1,0:T(8,128)(2,1)}, bf16[720,256]{1,0:T(8,128)(2,1)S(1)}) custom-call(f32[50,80,128]{2,1,0:T(8,128)S(1)} %noise.1.refs_0_, f32[16,24,128]{2,1,0:T(8,128)S(1)} %all-to-all-done.refs_1_, f32[16,128]{1,0:T(8,128)S(1)} %copy-done.1, f32[75,75]{1,0:T(8,128)S(1)} %copy-done), custom_call_target="tpu_custom_call" | custom-call | tf_op jit(solution)/shard_map/field/pallas_call | solution.py:283
  28.8 4.1 %all-to-all-start.1 = ((bf16[16,75,128]{2,1,0:T(8,128)(2,1)}), bf16[16,75,128]{2,1,0:T(8,128)(2,1)S(1)}, u32[]{:S(2)}, u32[]{:S(2)}) async-start(bf16[16,75,128]{2,1,0:T(8,128)(2,1)} %get-tuple-element.9), calls=%async_computation.1 | async-start | bytes 655360 | tf_op jit(solution)/shard_map/all_to_all | solution.py:303
  33.0 1.1 %weave.1 = bf16[75,8,256]{2,1,0:T(8,128)(2,1)} custom-call(bf16[720,256]{1,0:T(8,128)(2,1)S(1)} %get-tuple-element.8.field_ref), custom_call_target="tpu_custom_call" | custom-call | tf_op jit(solution)/shard_map/weave/pallas_call | solution.py:305
  34.1 9.7 %all-to-all-done.1 = bf16[16,75,128]{2,1,0:T(8,128)(2,1)S(1)} async-done(((bf16[16,75,128]{2,1,0:T(8,128)(2,1)}), bf16[16,75,128]{2,1,0:T(8,128)(2,1)S(1)}, u32[]{:S(2)}, u32[]{:S(2)}) %all-to-all-start.1) | async-done | bytes 307232 | tf_op jit(solution)/shard_map/all_to_all | solution.py:303
  43.8 0.8 %copy.10 = bf16[1,16,75,128]{3,1,2,0:T(8,128)(2,1)} copy(bf16[1,16,75,128]{3,2,1,0:T(8,128)(2,1)S(1)} %bitcast.3) | data formatting | bytes 614400
Async XLA Ops:
  0.6 17.5 %copy-start = (f32[75,75]{1,0:T(8,128)S(1)}, f32[75,75]{1,0:T(8,128)}, u32[]{:S(2)}) copy-start(f32[75,75]{1,0:T(8,128)} %refs_3_.1) | copy-start | bytes 67504
  2.4 15.8 %copy-start.1 = (f32[16,128]{1,0:T(8,128)S(1)}, f32[16,128]{1,0:T(8,128)}, u32[]{:S(2)}) copy-start(f32[16,128]{1,0:T(8,128)} %get-tuple-element.7.refs_2_) | copy-start | bytes 24580
  2.4 15.8 %all-to-all-start = ((f32[16,24,128]{2,1,0:T(8,128)}), f32[16,24,128]{2,1,0:T(8,128)S(1)}, u32[]{:S(2)}, u32[]{:S(2)}) async-start(f32[16,24,128]{2,1,0:T(8,128)} %get-tuple-element.6), calls=%async_computation | async-start | bytes 393216 | tf_op jit(solution)/shard_map/all_to_all | solution.py:271
  9.8 0.7 %copy-start.2 = (s32[2]{0:T(128)S(1)}, s32[2]{0:T(128)}, u32[]{:S(2)}) copy-start(s32[2]{0:T(128)} %refs_0_.1) | copy-start | bytes 28
  28.8 15.0 %all-to-all-start.1 = ((bf16[16,75,128]{2,1,0:T(8,128)(2,1)}), bf16[16,75,128]{2,1,0:T(8,128)(2,1)S(1)}, u32[]{:S(2)}, u32[]{:S(2)}) async-start(bf16[16,75,128]{2,1,0:T(8,128)(2,1)} %get-tuple-element.9), calls=%async_computation.1 | async-start | bytes 655360 | tf_op jit(solution)/shard_map/all_to_all | solution.py:303

commit v3 on v2

v3 whole, which is shorter than its diff:
```python
import jax
import jax.numpy as jnp
from jax import lax
from jax.experimental import pallas as pl
from jax.experimental.pallas import tpu as pltpu
from jax.sharding import PartitionSpec as P

STEPS = 8
LANES = 128
SUB = 8
EXACT = lax.Precision.HIGHEST
F32 = jnp.float32
BF16 = jnp.bfloat16
WAYS = 4
UNROLL = 2
I32 = jnp.int32
GOLDEN = -1640531535
ROOT12 = 3.4641016151377544
VMEM = pl.BlockSpec(memory_space=pltpu.VMEM)
SMEM = pl.BlockSpec(memory_space=pltpu.SMEM)
LIMIT = pltpu.CompilerParams(vmem_limit_bytes=24 << 20)


def resident(array):
    return pltpu.with_memory_space_constraint(array, pltpu.VMEM)


def up(value, unit):
    return -(-value // unit) * unit


def wrapped(value):
    return (value + 2**31) % 2**32 - 2**31


def iota(shape, axis):
    return lax.broadcasted_iota(I32, shape, axis)


def column_of(place, columns):
    run = columns // WAYS
    turn = sum(((place >= k * run).astype(I32) for k in range(1, WAYS)), jnp.zeros_like(place))
    return WAYS * (place - turn * run) + turn


def pack_kernel(
    diff_ref, wet_ref, norm_ref, cell_ref, frac_ref, count_ref, out_ref, kappa_out, norm_out
):
    tile_rows, columns = diff_ref.shape
    owners = cell_ref.shape[0]
    kappa = diff_ref[...] * wet_ref[...].astype(F32)
    square = (columns, columns)
    parting = (iota(square, 0) == column_of(iota(square, 1), columns)).astype(F32)
    both = jnp.concatenate([kappa, norm_ref[...]], 0)
    parted = jnp.dot(both, parting, precision=EXACT, preferred_element_type=F32)
    kappa_out[...] = parted[:tile_rows]
    norm_out[...] = parted[tile_rows:]
    parts = columns // LANES
    halo = jnp.concatenate(
        [parted[:tile_rows, k * LANES : (k + 1) * LANES] for k in range(parts)], 0
    ).astype(BF16)
    norms = [parted[tile_rows : tile_rows + 1, k * LANES : (k + 1) * LANES] for k in range(parts)]
    cell = cell_ref[...]
    row = jnp.zeros_like(cell)
    for step in range(1, tile_rows):
        row = row + (cell >= step * columns).astype(I32)
    col = (cell - row * columns).astype(F32)
    row = row.astype(F32)
    frac_y, frac_x = frac_ref[:, 0, :], frac_ref[:, 1, :]
    high_y, high_x = (frac.astype(BF16).astype(F32) for frac in (frac_y, frac_x))
    low_y, low_x = frac_y - high_y, frac_x - high_x
    lane = iota((1, LANES), 1)
    for owner in range(owners):
        at = slice(owner, owner + 1)
        live = lane < count_ref[0, owner]
        tail = jnp.concatenate(
            norms + [col[at], high_x[at], low_x[at]]
            + [jnp.where(live, row[at], -16.0), high_y[at], low_y[at]],
            0,
        )
        out_ref[owner, : parts * tile_rows, :] = halo
        out_ref[owner, parts * tile_rows :, :] = tail.astype(BF16)


def mix(hashed):
    hashed = (hashed ^ lax.shift_right_logical(hashed, 16)) * -2048144789
    hashed = (hashed ^ lax.shift_right_logical(hashed, 13)) * -1028477387
    hashed = hashed ^ lax.shift_right_logical(hashed, 16)
    return hashed


def noise_kernel(total_rows, tile_rows, columns, seed_ref, out_ref):
    planes, height, _ = out_ref.shape
    run = columns // WAYS
    groups = LANES // run
    first_row = lax.axis_index("tile") * tile_rows - STEPS
    step_level = wrapped(total_rows * columns * GOLDEN)
    shape = (SUB, LANES)
    group = sum(((iota(shape, 1) >= g * run).astype(I32) for g in range(1, groups)), 0)
    base = (iota(shape, 0) + SUB * group) * step_level
    base = base + (iota(shape, 1) - group * run) * wrapped(WAYS * GOLDEN)
    gain = ROOT12 / 16777216.0
    shift = (0.5 / 16777216.0 - 0.5) * ROOT12
    origin = first_row * wrapped(columns * GOLDEN) + seed_ref[0]
    second = seed_ref[1]

    def one_tile(part, carry):
        start = origin + part * wrapped(groups * SUB * step_level)
        span = pl.ds(pl.multiple_of(part * SUB, SUB), SUB)
        for plane in range(planes):
            offset = start + wrapped(((plane // WAYS) * columns + plane % WAYS) * GOLDEN)
            hashed = mix(mix(base + offset) ^ second)
            drawn = lax.shift_right_logical(hashed, 8).astype(F32)
            out_ref[plane, span, :] = drawn * gain + shift
        return carry

    lax.fori_loop(0, height // SUB, one_tile, 0)


def field_kernel(
    tiles, noise_ref, recv_ref, kappa_ref, norm_ref, vert_ref, prof_ref, field_ref,
    halo_ref, root_ref, keep_ref, gain_ref, vert_pad, state_ref,
):
    planes, height, _ = noise_ref.shape
    rows = planes // WAYS
    tile_rows, columns = norm_ref.shape
    run = columns // WAYS
    groups = LANES // run
    levels = height * groups
    depth = vert_ref.shape[0]
    out_rows = tile_rows + 1
    parts = columns // LANES
    tile = lax.axis_index("tile")

    halo_ref[...] = jnp.zeros_like(halo_ref)
    halo_ref[tile_rows : 2 * tile_rows] = kappa_ref[...]
    for place, shift, count in ((0, -1, tile_rows), (2, 1, tile_rows), (3, 2, 1)):
        source = tile + shift
        valid = ((source >= 0) & (source < tiles)).astype(F32)
        given = recv_ref[jnp.clip(source, 0, tiles - 1), : parts * tile_rows, :].astype(F32) * valid
        for k in range(parts):
            halo_ref[place * tile_rows : place * tile_rows + count, k * LANES : (k + 1) * LANES] = (
                given[k * tile_rows : k * tile_rows + count]
            )
    root = jnp.sqrt(halo_ref[...])
    lane = iota((1, LANES), 1)
    roots = []
    for k in range(WAYS):
        vector = root[:, (k // groups) * LANES : (k // groups + 1) * LANES]
        turned = pltpu.roll(vector, run, 1)
        keeps = (lane >= run) if k % groups else (lane < run)
        roots.append(jnp.where(keeps, vector, turned))
        root_ref[k] = roots[k]
    edge_low, edge_high = (lane == 0) | (lane == run), (lane == run - 1) | (lane == LANES - 1)
    inner = slice(1, rows - 1)
    for k in range(WAYS):
        west = roots[k - 1] if k else jnp.where(edge_low, 0.0, pltpu.roll(roots[-1], 1, 1))
        east = (
            roots[k + 1]
            if k < WAYS - 1
            else jnp.where(edge_high, 0.0, pltpu.roll(roots[0], LANES - 1, 1))
        )
        near = root_ref[k, : rows - 2] + root_ref[k, 2:rows] + (west + east)[inner]
        keep_ref[k, inner] = 1.0 - roots[k][inner] * near
        gain_ref[k, inner] = roots[k][inner] * roots[k][inner]
    kappa = halo_ref[STEPS : STEPS + out_rows]
    wet = kappa > 0.0
    inverse = jnp.where(wet, root[STEPS : STEPS + out_rows] / jnp.where(wet, kappa, 1.0), 0.0)
    below = recv_ref[jnp.clip(tile + 1, 0, tiles - 1), parts * tile_rows :, :].astype(F32)
    norm_below = jnp.concatenate([below[k : k + 1] for k in range(parts)], 1)
    scales = inverse * jnp.concatenate([norm_ref[...], norm_below], 0)

    block = (SUB, LANES)
    lanes = iota(block, 1)
    low8, high8 = (lanes == 0) | (lanes == run), (lanes == run - 1) | (lanes == LANES - 1)
    lower = lanes < run

    def spread(ref, k, row):
        return ref[k, pl.ds(row, SUB, stride=0), :]

    def diffuse(part, carry):
        span = pl.ds(pl.multiple_of(part * SUB, SUB), SUB)
        out_span = pl.ds(pl.multiple_of(part * groups * SUB, groups * SUB), groups * SUB)
        low_span = pl.ds(pl.multiple_of(levels + part * groups * SUB, groups * SUB), groups * SUB)
        again = pl.ds(pl.multiple_of(2 * levels + part * groups * SUB, groups * SUB), groups * SUB)
        known = [{} for _ in range(STEPS + 1)]
        for top in range(rows):
            known[0][top] = [
                noise_ref[WAYS * top + k, span, :] * spread(root_ref, k, top) for k in range(WAYS)
            ]
            for step in range(1, STEPS + 1):
                row = top - step
                if row < step:
                    break
                past = known[step - 1]
                here = past[row]
                fresh = []
                for k in range(WAYS):
                    west = here[k - 1] if k else jnp.where(low8, 0.0, pltpu.roll(here[-1], 1, 1))
                    east = (
                        here[k + 1]
                        if k < WAYS - 1
                        else jnp.where(high8, 0.0, pltpu.roll(here[0], LANES - 1, 1))
                    )
                    near = (past[row - 1][k] + past[row + 1][k]) + (west + east)
                    fresh.append(spread(keep_ref, k, row) * here[k] + spread(gain_ref, k, row) * near)
                known[step][row] = fresh
                del past[row - 1]
        for row in range(out_rows):
            done = known[STEPS][STEPS + row]
            for k in range(parts):
                one, two = done[2 * k], done[2 * k + 1]
                low = jnp.where(lower, one, pltpu.roll(two, run, 1))
                high = jnp.where(lower, pltpu.roll(one, run, 1), two)
                state = jnp.concatenate([low, high], 0)
                head = state.astype(BF16)
                at = slice(row * columns + k * LANES, row * columns + (k + 1) * LANES)
                state_ref[out_span, at] = head
                state_ref[low_span, at] = (state - head.astype(F32)).astype(BF16)
                state_ref[again, at] = head
        return carry

    lax.fori_loop(0, height // SUB, diffuse, 0)

    vert_pad[...] = jnp.zeros_like(vert_pad)
    vert_pad[:depth, :depth] = vert_ref[...]
    vert = vert_pad[...]
    head = vert.astype(BF16).astype(F32)
    factor = head + pltpu.roll(head, levels, 1) + pltpu.roll(vert - head, 2 * levels, 1)
    factor = factor.astype(BF16)[:, : 3 * levels]
    for row in range(out_rows):
        mixed = jnp.dot(
            factor,
            state_ref[:, row * columns : (row + 1) * columns],
            preferred_element_type=F32,
        )
        scaled = (mixed * scales[row : row + 1]).astype(BF16)
        field_ref[row * levels : (row + 1) * levels, :] = scaled

    col = column_of(iota((columns, 2 * LANES), 0), columns).astype(F32)

    def interpolate(pair, carry):
        tails = [recv_ref[2 * pair + k, parts * tile_rows :, :].astype(F32) for k in range(2)]
        tail = jnp.concatenate(tails, 1)
        pos_x = tail[parts : parts + 1] + (tail[parts + 1 : parts + 2] + tail[parts + 2 : parts + 3])
        pos_y = tail[parts + 3 : parts + 4] + (tail[parts + 4 : parts + 5] + tail[parts + 5 : parts + 6])
        hat = jnp.maximum(1.0 - jnp.abs(pos_x - col), 0.0).astype(BF16)
        total = None
        for row in range(out_rows):
            along = jnp.dot(
                field_ref[row * levels : (row + 1) * levels, :], hat, preferred_element_type=F32
            )
            weight = jnp.maximum(1.0 - jnp.abs(pos_y - float(row)), 0.0)
            total = along * weight if total is None else total + along * weight
        rounded = total[:depth].astype(BF16)
        prof_ref[2 * pair] = rounded[:, :LANES]
        prof_ref[2 * pair + 1] = rounded[:, LANES:]
        return carry

    lax.fori_loop(0, tiles // 2, interpolate, 0, unroll=UNROLL)


def weave_kernel(field_ref, out_ref, flat_ref):
    depth, tile_rows, columns = out_ref.shape
    levels = field_ref.shape[0] // (tile_rows + 1)
    square = (columns, columns)
    weave = (iota(square, 1) == column_of(iota(square, 0), columns)).astype(BF16)
    for row in range(tile_rows):
        woven = jnp.dot(
            field_ref[row * levels : (row + 1) * levels, :], weave, preferred_element_type=F32
        )
        flat_ref[:, row, :] = woven
    out_ref[...] = flat_ref[:depth].astype(BF16)


def body(
    noise_seeds, diffusivity, wet_mask, vert_factor, norm_scale, obs_cell, obs_frac, obs_count
):
    tile_rows, columns = diffusivity.shape
    depth = vert_factor.shape[0]
    levels = up(depth, 2 * SUB)
    tiles = lax.axis_size("tile")
    total_rows = tile_rows * tiles
    groups = LANES * WAYS // columns
    rows = tile_rows + 1 + 2 * STEPS
    slots = obs_cell.shape[2]
    parts = columns // LANES
    square = jax.ShapeDtypeStruct((tile_rows, columns), F32)

    packed, kappa_split, norm_split = pl.pallas_call(
        pack_kernel,
        out_shape=(
            jax.ShapeDtypeStruct((tiles, parts * tile_rows + SUB, LANES), BF16),
            square,
            square,
        ),
        in_specs=[VMEM] * 5 + [SMEM],
        out_specs=(VMEM,) * 3,
        name="pack",
    )(diffusivity, wet_mask, norm_scale, obs_cell[0], obs_frac[0], obs_count)
    received = lax.all_to_all(packed, "tile", split_axis=0, concat_axis=0, tiled=True)

    noise = pl.pallas_call(
        lambda *refs: noise_kernel(total_rows, tile_rows, columns, *refs),
        out_shape=pltpu.VMEM((WAYS * rows, levels // groups, LANES), F32),
        in_specs=[SMEM],
        out_specs=VMEM,
        name="noise",
        compiler_params=LIMIT,
    )(noise_seeds)

    coefficients = pltpu.VMEM((WAYS, up(rows, SUB), LANES), F32)
    answers, field = pl.pallas_call(
        lambda *refs: field_kernel(tiles, *refs),
        out_shape=(
            jax.ShapeDtypeStruct((tiles, depth, slots), BF16),
            pltpu.VMEM(((tile_rows + 1) * levels, columns), BF16),
        ),
        in_specs=[VMEM] * 5,
        out_specs=(VMEM, VMEM),
        scratch_shapes=[
            pltpu.VMEM((up(rows, SUB), columns), F32),
            coefficients,
            coefficients,
            coefficients,
            pltpu.VMEM((levels, up(3 * levels, LANES)), F32),
            pltpu.VMEM((3 * levels, (tile_rows + 1) * columns), BF16),
        ],
        name="field",
        compiler_params=LIMIT,
    )(resident(noise), resident(received), resident(kappa_split), resident(norm_split), vert_factor)
    profiles = lax.all_to_all(answers, "tile", split_axis=0, concat_axis=0, tiled=True)

    perturbation = pl.pallas_call(
        weave_kernel,
        out_shape=jax.ShapeDtypeStruct((depth, tile_rows, columns), BF16),
        in_specs=[VMEM],
        out_specs=VMEM,
        scratch_shapes=[pltpu.VMEM((levels, tile_rows, columns), F32)],
        name="weave",
        compiler_params=LIMIT,
    )(resident(field))
    return (perturbation, profiles[None])


def solution(mesh):
    in_specs = (
        P("member"),
        P("tile", None),
        P("tile", None),
        P(),
        P("tile", None),
        P("tile", None, None),
        P("tile", None, None, None),
        P("tile", None),
    )
    out_specs = (P("member", "tile", None), P("tile", None, "member", None))
    return jax.shard_map(body, mesh=mesh, in_specs=in_specs, out_specs=out_specs, check_vma=False)
```

time: 45.4 us -> 40.6 us (0.89)
  Pallas kernels: 15.8 us -> 12.5 us
  waiting for transfers between devices: 15.1 us -> 13.3 us
    pallas_call x1, Pallas kernels: 10.7 us -> 7.49 us  [body(): pl.pallas_call(lambda *refs: field_kernel(tiles, *refs), out_shape=(jax.S...]
    all_to_all x1, waiting for transfers between devices: 5.38 us -> 3.6 us  [body(): lax.all_to_all(packed, 'tile', split_axis=0, concat_axis=0, tiled=True)]
    unnamed x7 -> x9, local copies, waits for them, and re-layouts: 1.45 us -> 1.46 us
where the time goes in v3:
time: 40.6 us; the launch traced here: 39.8 us
  waiting for transfers between devices  13.3 us (33%)
  Pallas kernels  12.5 us (31%)
  starting transfers between devices  11.9 us (29%)
  local copies, waits for them, and re-layouts  1.46 us (4%)
  between operations  0.66 us (2%)
    all_to_all x1, waiting for transfers between devices, body(): lax.all_to_all(answers, 'tile', split_axis=0, concat_axis=0, tiled=True)  9.72 us
    pallas_call x1, Pallas kernels, body(): pl.pallas_call(lambda *refs: field_kernel(tiles, *refs), out_shape=(jax.S...  7.49 us
    all_to_all x1, starting transfers between devices, body(): lax.all_to_all(packed, 'tile', split_axis=0, concat_axis=0, tiled=True)  7.48 us
    all_to_all x1, starting transfers between devices, body(): lax.all_to_all(answers, 'tile', split_axis=0, concat_axis=0, tiled=True)  4.41 us
    all_to_all x1, waiting for transfers between devices, body(): lax.all_to_all(packed, 'tile', split_axis=0, concat_axis=0, tiled=True)  3.6 us
    pallas_call x1, Pallas kernels, body(): pl.pallas_call(lambda *refs: noise_kernel(total_rows, tile_rows, columns,...  2.13 us
    pallas_call x1, Pallas kernels, body(): pl.pallas_call(pack_kernel, out_shape=(jax.ShapeDtypeStruct((tiles, parts...  1.71 us
    unnamed x9, local copies, waits for them, and re-layouts  1.46 us
  transfers between devices with their start and end apart: 2, of which 2 were waited for; matrix products, arithmetic and copies ran while one was open for 0% of the time, Pallas kernels for 8%

profile of v3, /device:TPU:1, one launch (start us, length us, event | category | flops | bytes accessed | tf_op | source)
XLA Modules:
  0.0 39.8 jit_solution(9459603102650243338)
XLA Ops:
  0.6 0.0 copy-start
  0.6 1.7 %pack.1 = (bf16[16,24,128]{2,1,0:T(8,128)(2,1)}, f32[8,256]{1,0:T(8,128)}, f32[8,256]{1,0:T(8,128)}) custom-call(f32[8,256]{1,0:T(8,128)} %diff_ref.1, s32[8,256]{1,0:T(8,128)} %wet_ref.1, f32[8,256]{1,0:T(8,128)} %norm_ref.1, s32[16,128]{1,0:T(8,128)} %bitcast.5, f32[16,2,128]{2,1,0:T(2,128)} %bitcast.4, s32[1,16]{1,0:T(1,128)} %count_ref.1), custom_call_target="tpu_custom_call" | custom-call | tf_op jit(solution)/shard_map/pack/pallas_call | solution.py:290
  2.4 0.0 copy-start.1
  2.4 0.0 copy-start.2
  2.4 7.5 %all-to-all-start = ((bf16[16,24,128]{2,1,0:T(8,128)(2,1)}), bf16[16,24,128]{2,1,0:T(8,128)(2,1)S(1)}, u32[]{:S(2)}, u32[]{:S(2)}) async-start(bf16[16,24,128]{2,1,0:T(8,128)(2,1)} %get-tuple-element.7), calls=%async_computation | async-start | bytes 196608 | tf_op jit(solution)/shard_map/all_to_all | solution.py:301
  9.8 0.0 copy-start.3
  9.8 0.6 %copy-done.3 = s32[2]{0:T(128)S(1)} copy-done((s32[2]{0:T(128)S(1)}, s32[2]{0:T(128)}, u32[]{:S(2)}) %copy-start.3) | copy-done | bytes 32
  10.5 2.1 %noise.1.refs_0_ = f32[100,40,128]{2,1,0:T(8,128)S(1)} custom-call(s32[2]{0:T(128)S(1)} %copy-done.3), custom_call_target="tpu_custom_call" | custom-call | tf_op jit(solution)/shard_map/noise/pallas_call | solution.py:303
  12.6 3.6 %all-to-all-done.refs_1_ = bf16[16,24,128]{2,1,0:T(8,128)(2,1)S(1)} async-done(((bf16[16,24,128]{2,1,0:T(8,128)(2,1)}), bf16[16,24,128]{2,1,0:T(8,128)(2,1)S(1)}, u32[]{:S(2)}, u32[]{:S(2)}) %all-to-all-start) | async-done | bytes 98336 | tf_op jit(solution)/shard_map/all_to_all | solution.py:301
  16.2 0.0 copy-done
  16.2 0.0 copy-done.1
  16.2 0.0 copy-done.2
  16.2 7.5 %field.1 = (bf16[16,75,128]{2,1,0:T(8,128)(2,1)}, bf16[720,256]{1,0:T(8,128)(2,1)S(1)}) custom-call(f32[100,40,128]{2,1,0:T(8,128)S(1)} %noise.1.refs_0_, bf16[16,24,128]{2,1,0:T(8,128)(2,1)S(1)} %all-to-all-done.refs_1_, f32[8,256]{1,0:T(8,128)S(1)} %copy-done.1, f32[8,256]{1,0:T(8,128)S(1)} %copy-done.2, f32[75,75]{1,0:T(8,128)S(1)} %copy-done), custom_call_target="tpu_custom_call" | custom-call | tf_op jit(solution)/shard_map/field/pallas_call | solution.py:313
  23.7 4.4 %all-to-all-start.1 = ((bf16[16,75,128]{2,1,0:T(8,128)(2,1)}), bf16[16,75,128]{2,1,0:T(8,128)(2,1)S(1)}, u32[]{:S(2)}, u32[]{:S(2)}) async-start(bf16[16,75,128]{2,1,0:T(8,128)(2,1)} %get-tuple-element.11), calls=%async_computation.1 | async-start | bytes 655360 | tf_op jit(solution)/shard_map/all_to_all | solution.py:332
  28.1 1.1 %weave.1 = bf16[75,8,256]{2,1,0:T(8,128)(2,1)} custom-call(bf16[720,256]{1,0:T(8,128)(2,1)S(1)} %get-tuple-element.10.field_ref), custom_call_target="tpu_custom_call" | custom-call | tf_op jit(solution)/shard_map/weave/pallas_call | solution.py:334
  29.3 9.7 %all-to-all-done.1 = bf16[16,75,128]{2,1,0:T(8,128)(2,1)S(1)} async-done(((bf16[16,75,128]{2,1,0:T(8,128)(2,1)}), bf16[16,75,128]{2,1,0:T(8,128)(2,1)S(1)}, u32[]{:S(2)}, u32[]{:S(2)}) %all-to-all-start.1) | async-done | bytes 307232 | tf_op jit(solution)/shard_map/all_to_all | solution.py:332
  39.0 0.8 %copy.10 = bf16[1,16,75,128]{3,1,2,0:T(8,128)(2,1)} copy(bf16[1,16,75,128]{3,2,1,0:T(8,128)(2,1)S(1)} %bitcast.3) | data formatting | bytes 614400
Async XLA Ops:
  0.6 15.6 %copy-start = (f32[75,75]{1,0:T(8,128)S(1)}, f32[75,75]{1,0:T(8,128)}, u32[]{:S(2)}) copy-start(f32[75,75]{1,0:T(8,128)} %refs_4_.1) | copy-start | bytes 67504
  2.4 13.9 %copy-start.1 = (f32[8,256]{1,0:T(8,128)S(1)}, f32[8,256]{1,0:T(8,128)}, u32[]{:S(2)}) copy-start(f32[8,256]{1,0:T(8,128)} %get-tuple-element.8.refs_2_) | copy-start | bytes 24580
  2.4 13.9 %copy-start.2 = (f32[8,256]{1,0:T(8,128)S(1)}, f32[8,256]{1,0:T(8,128)}, u32[]{:S(2)}) copy-start(f32[8,256]{1,0:T(8,128)} %get-tuple-element.9.refs_3_) | copy-start | bytes 24580
  2.4 13.9 %all-to-all-start = ((bf16[16,24,128]{2,1,0:T(8,128)(2,1)}), bf16[16,24,128]{2,1,0:T(8,128)(2,1)S(1)}, u32[]{:S(2)}, u32[]{:S(2)}) async-start(bf16[16,24,128]{2,1,0:T(8,128)(2,1)} %get-tuple-element.7), calls=%async_computation | async-start | bytes 196608 | tf_op jit(solution)/shard_map/all_to_all | solution.py:301
  9.8 0.7 %copy-start.3 = (s32[2]{0:T(128)S(1)}, s32[2]{0:T(128)}, u32[]{:S(2)}) copy-start(s32[2]{0:T(128)} %refs_0_.1) | copy-start | bytes 28
  23.7 15.3 %all-to-all-start.1 = ((bf16[16,75,128]{2,1,0:T(8,128)(2,1)}), bf16[16,75,128]{2,1,0:T(8,128)(2,1)S(1)}, u32[]{:S(2)}, u32[]{:S(2)}) async-start(bf16[16,75,128]{2,1,0:T(8,128)(2,1)} %get-tuple-element.11), calls=%async_computation.1 | async-start | bytes 655360 | tf_op jit(solution)/shard_map/all_to_all | solution.py:332

commit v4 on v3

--- a/solution.py
+++ b/solution.py
@@ -12,7 +12,8 @@
 F32 = jnp.float32
 BF16 = jnp.bfloat16
 WAYS = 4
-UNROLL = 2
+TOGETHER = 5
+PAIRS = 8
 I32 = jnp.int32
 GOLDEN = -1640531535
 ROOT12 = 3.4641016151377544
@@ -37,6 +38,18 @@
     return lax.broadcasted_iota(I32, shape, axis)
 
 
+def visiting_order(tiles):
+    pairs = tiles // 2
+    ring = list(range(1, pairs, 2)) + list(range(0, pairs, 2))[::-1]
+    turn = pairs // 4
+    return [2 * pair + core for pair in ring[turn:] + ring[:turn] for core in (1, 0)]
+
+
+def place_of(tile, tiles):
+    order = visiting_order(tiles)
+    return sum(jnp.where(tile == order[place], place, 0) for place in range(1, tiles))
+
+
 def column_of(place, columns):
     run = columns // WAYS
     turn = sum(((place >= k * run).astype(I32) for k in range(1, WAYS)), jnp.zeros_like(place))
@@ -48,6 +61,7 @@
 ):
     tile_rows, columns = diff_ref.shape
     owners = cell_ref.shape[0]
+    order = visiting_order(owners)
     kappa = diff_ref[...] * wet_ref[...].astype(F32)
     square = (columns, columns)
     parting = (iota(square, 0) == column_of(iota(square, 1), columns)).astype(F32)
@@ -78,8 +92,9 @@
             + [jnp.where(live, row[at], -16.0), high_y[at], low_y[at]],
             0,
         )
-        out_ref[owner, : parts * tile_rows, :] = halo
-        out_ref[owner, parts * tile_rows :, :] = tail.astype(BF16)
+        at = order.index(owner)
+        out_ref[at, : parts * tile_rows, :] = halo
+        out_ref[at, parts * tile_rows :, :] = tail.astype(BF16)
 
 
 def mix(hashed):
@@ -119,7 +134,7 @@
 
 def field_kernel(
     tiles, noise_ref, recv_ref, kappa_ref, norm_ref, vert_ref, prof_ref, field_ref,
-    halo_ref, root_ref, keep_ref, gain_ref, vert_pad, state_ref,
+    halo_ref, root_ref, keep_ref, gain_ref, vert_pad, state_ref, hat_ref,
 ):
     planes, height, _ = noise_ref.shape
     rows = planes // WAYS
@@ -137,7 +152,7 @@
     for place, shift, count in ((0, -1, tile_rows), (2, 1, tile_rows), (3, 2, 1)):
         source = tile + shift
         valid = ((source >= 0) & (source < tiles)).astype(F32)
-        given = recv_ref[jnp.clip(source, 0, tiles - 1), : parts * tile_rows, :].astype(F32) * valid
+        given = recv_ref[place_of(jnp.clip(source, 0, tiles - 1), tiles), : parts * tile_rows, :].astype(F32) * valid
         for k in range(parts):
             halo_ref[place * tile_rows : place * tile_rows + count, k * LANES : (k + 1) * LANES] = (
                 given[k * tile_rows : k * tile_rows + count]
@@ -166,7 +181,7 @@
     kappa = halo_ref[STEPS : STEPS + out_rows]
     wet = kappa > 0.0
     inverse = jnp.where(wet, root[STEPS : STEPS + out_rows] / jnp.where(wet, kappa, 1.0), 0.0)
-    below = recv_ref[jnp.clip(tile + 1, 0, tiles - 1), parts * tile_rows :, :].astype(F32)
+    below = recv_ref[place_of(jnp.clip(tile + 1, 0, tiles - 1), tiles), parts * tile_rows :, :].astype(F32)
     norm_below = jnp.concatenate([below[k : k + 1] for k in range(parts)], 1)
     scales = inverse * jnp.concatenate([norm_ref[...], norm_below], 0)
 
@@ -178,49 +193,64 @@
     def spread(ref, k, row):
         return ref[k, pl.ds(row, SUB, stride=0), :]
 
-    def diffuse(part, carry):
-        span = pl.ds(pl.multiple_of(part * SUB, SUB), SUB)
-        out_span = pl.ds(pl.multiple_of(part * groups * SUB, groups * SUB), groups * SUB)
-        low_span = pl.ds(pl.multiple_of(levels + part * groups * SUB, groups * SUB), groups * SUB)
-        again = pl.ds(pl.multiple_of(2 * levels + part * groups * SUB, groups * SUB), groups * SUB)
+    def diffuse(bundle, carry):
+        spans = [
+            pl.ds(pl.multiple_of((bundle * TOGETHER + part) * SUB, SUB), SUB) for part in range(TOGETHER)
+        ]
         known = [{} for _ in range(STEPS + 1)]
+
+        def drawn(row):
+            cells = []
+            for k in range(WAYS):
+                scale = spread(root_ref, k, row)
+                cells.append([noise_ref[WAYS * row + k, span, :] * scale for span in spans])
+            return cells
+
+        def stepped(past, row):
+            here, fresh = past[row], []
+            for k in range(WAYS):
+                keep, gain = spread(keep_ref, k, row), spread(gain_ref, k, row)
+                cells = []
+                for part in range(TOGETHER):
+                    if k:
+                        west = here[k - 1][part]
+                    else:
+                        west = jnp.where(low8, 0.0, pltpu.roll(here[-1][part], 1, 1))
+                    if k < WAYS - 1:
+                        east = here[k + 1][part]
+                    else:
+                        east = jnp.where(high8, 0.0, pltpu.roll(here[0][part], LANES - 1, 1))
+                    near = (past[row - 1][k][part] + past[row + 1][k][part]) + (west + east)
+                    cells.append(keep * here[k][part] + gain * near)
+                fresh.append(cells)
+            return fresh
+
         for top in range(rows):
-            known[0][top] = [
-                noise_ref[WAYS * top + k, span, :] * spread(root_ref, k, top) for k in range(WAYS)
-            ]
+            known[0][top] = drawn(top)
             for step in range(1, STEPS + 1):
                 row = top - step
                 if row < step:
                     break
-                past = known[step - 1]
-                here = past[row]
-                fresh = []
-                for k in range(WAYS):
-                    west = here[k - 1] if k else jnp.where(low8, 0.0, pltpu.roll(here[-1], 1, 1))
-                    east = (
-                        here[k + 1]
-                        if k < WAYS - 1
-                        else jnp.where(high8, 0.0, pltpu.roll(here[0], LANES - 1, 1))
-                    )
-                    near = (past[row - 1][k] + past[row + 1][k]) + (west + east)
-                    fresh.append(spread(keep_ref, k, row) * here[k] + spread(gain_ref, k, row) * near)
-                known[step][row] = fresh
-                del past[row - 1]
+                known[step][row] = stepped(known[step - 1], row)
+                del known[step - 1][row - 1]
         for row in range(out_rows):
-            done = known[STEPS][STEPS + row]
+            done = known[STEPS][row + STEPS]
             for k in range(parts):
-                one, two = done[2 * k], done[2 * k + 1]
-                low = jnp.where(lower, one, pltpu.roll(two, run, 1))
-                high = jnp.where(lower, pltpu.roll(one, run, 1), two)
-                state = jnp.concatenate([low, high], 0)
-                head = state.astype(BF16)
-                at = slice(row * columns + k * LANES, row * columns + (k + 1) * LANES)
-                state_ref[out_span, at] = head
-                state_ref[low_span, at] = (state - head.astype(F32)).astype(BF16)
-                state_ref[again, at] = head
+                for part in range(TOGETHER):
+                    one, two = done[2 * k][part], done[2 * k + 1][part]
+                    low = jnp.where(lower, one, pltpu.roll(two, run, 1))
+                    high = jnp.where(lower, pltpu.roll(one, run, 1), two)
+                    state = jnp.concatenate([low, high], 0)
+                    head = state.astype(BF16)
+                    tail = (state - head.astype(F32)).astype(BF16)
+                    first = row * columns + k * LANES
+                    for place, piece in enumerate((head, tail, head)):
+                        start = place * levels + (bundle * TOGETHER + part) * 2 * SUB
+                        at = pl.ds(pl.multiple_of(start, 2 * SUB), 2 * SUB)
+                        state_ref[at, first : first + LANES] = piece
         return carry
 
-    lax.fori_loop(0, height // SUB, diffuse, 0)
+    lax.fori_loop(0, height // SUB // TOGETHER, diffuse, 0)
 
     vert_pad[...] = jnp.zeros_like(vert_pad)
     vert_pad[:depth, :depth] = vert_ref[...]
@@ -228,6 +258,7 @@
     head = vert.astype(BF16).astype(F32)
     factor = head + pltpu.roll(head, levels, 1) + pltpu.roll(vert - head, 2 * levels, 1)
     factor = factor.astype(BF16)[:, : 3 * levels]
+    bunch = 2 * SUB
     for row in range(out_rows):
         mixed = jnp.dot(
             factor,
@@ -235,29 +266,43 @@
             preferred_element_type=F32,
         )
         scaled = (mixed * scales[row : row + 1]).astype(BF16)
-        field_ref[row * levels : (row + 1) * levels, :] = scaled
+        for part in range(levels // bunch):
+            first = (part * out_rows + row) * bunch
+            field_ref[first : first + bunch, :] = scaled[part * bunch : (part + 1) * bunch]
 
     col = column_of(iota((columns, 2 * LANES), 0), columns).astype(F32)
 
-    def interpolate(pair, carry):
+    def positions(pair, first):
         tails = [recv_ref[2 * pair + k, parts * tile_rows :, :].astype(F32) for k in range(2)]
         tail = jnp.concatenate(tails, 1)
-        pos_x = tail[parts : parts + 1] + (tail[parts + 1 : parts + 2] + tail[parts + 2 : parts + 3])
-        pos_y = tail[parts + 3 : parts + 4] + (tail[parts + 4 : parts + 5] + tail[parts + 5 : parts + 6])
-        hat = jnp.maximum(1.0 - jnp.abs(pos_x - col), 0.0).astype(BF16)
-        total = None
-        for row in range(out_rows):
-            along = jnp.dot(
-                field_ref[row * levels : (row + 1) * levels, :], hat, preferred_element_type=F32
-            )
-            weight = jnp.maximum(1.0 - jnp.abs(pos_y - float(row)), 0.0)
-            total = along * weight if total is None else total + along * weight
-        rounded = total[:depth].astype(BF16)
-        prof_ref[2 * pair] = rounded[:, :LANES]
-        prof_ref[2 * pair + 1] = rounded[:, LANES:]
+        return tail[first : first + 1] + (tail[first + 1 : first + 2] + tail[first + 2 : first + 3])
+
+    def make_hat(pair, slot):
+        hat_ref[slot] = jnp.maximum(1.0 - jnp.abs(positions(pair, parts) - col), 0.0).astype(BF16)
+
+    def answer(pair, hat):
+        along = jnp.dot(field_ref[...], hat, preferred_element_type=F32)
+        pos_y = positions(pair, parts + 3)
+        weights = [jnp.maximum(1.0 - jnp.abs(pos_y - float(row)), 0.0) for row in range(out_rows)]
+        for part in range(levels // bunch):
+            total = None
+            for row in range(out_rows):
+                first = (part * out_rows + row) * bunch
+                term = along[first : first + bunch] * weights[row]
+                total = term if total is None else total + term
+            kept = min(bunch, depth - part * bunch)
+            rounded = total.astype(BF16)[:kept]
+            prof_ref[2 * pair, part * bunch : part * bunch + kept, :] = rounded[:, :LANES]
+            prof_ref[2 * pair + 1, part * bunch : part * bunch + kept, :] = rounded[:, LANES:]
+
+    def some_pairs(step, carry):
+        for slot in range(PAIRS):
+            make_hat(step * PAIRS + slot, slot)
+        for slot in range(PAIRS):
+            answer(step * PAIRS + slot, hat_ref[slot])
         return carry
 
-    lax.fori_loop(0, tiles // 2, interpolate, 0, unroll=UNROLL)
+    lax.fori_loop(0, tiles // (2 * PAIRS), some_pairs, 0)
 
 
 def weave_kernel(field_ref, out_ref, flat_ref):
@@ -265,12 +310,30 @@
     levels = field_ref.shape[0] // (tile_rows + 1)
     square = (columns, columns)
     weave = (iota(square, 1) == column_of(iota(square, 0), columns)).astype(BF16)
-    for row in range(tile_rows):
-        woven = jnp.dot(
-            field_ref[row * levels : (row + 1) * levels, :], weave, preferred_element_type=F32
+    woven = jnp.dot(field_ref[...], weave, preferred_element_type=F32)
+    bunch = 2 * SUB
+    for part in range(levels // bunch):
+        for row in range(tile_rows):
+            first = (part * (tile_rows + 1) + row) * bunch
+            flat_ref[part * bunch : (part + 1) * bunch, row, :] = woven[first : first + bunch]
+    out_ref[...] = flat_ref[:depth].astype(BF16)
+
+
+def unpack_kernel(order, given_ref, out_ref, wide_ref, ready_ref, sems):
+    depth = given_ref.shape[1]
+    bunch = 2 * SUB
+    copies = []
+    for part, start in enumerate(range(0, depth, bunch)):
+        stop = min(start + bunch, depth)
+        for place, owner in enumerate(order):
+            wide_ref[start:stop, owner, :] = given_ref[place, start:stop, :].astype(F32)
+        ready_ref[start:stop] = wide_ref[start:stop].astype(BF16)
+        copies.append(
+            pltpu.make_async_copy(ready_ref.at[start:stop], out_ref.at[start:stop], sems.at[part])
         )
-        flat_ref[:, row, :] = woven
-    out_ref[...] = flat_ref[:depth].astype(BF16)
+        copies[-1].start()
+    for copy in copies:
+        copy.wait()
 
 
 def body(
@@ -298,7 +361,11 @@
         out_specs=(VMEM,) * 3,
         name="pack",
     )(diffusivity, wet_mask, norm_scale, obs_cell[0], obs_frac[0], obs_count)
-    received = lax.all_to_all(packed, "tile", split_axis=0, concat_axis=0, tiled=True)
+    order = visiting_order(tiles)
+    exchange = dict(
+        axis_name="tile", split_axis=0, concat_axis=0, tiled=True, axis_index_groups=[order]
+    )
+    received = lax.all_to_all(packed, **exchange)
 
     noise = pl.pallas_call(
         lambda *refs: noise_kernel(total_rows, tile_rows, columns, *refs),
@@ -325,12 +392,12 @@
             coefficients,
             pltpu.VMEM((levels, up(3 * levels, LANES)), F32),
             pltpu.VMEM((3 * levels, (tile_rows + 1) * columns), BF16),
+            pltpu.VMEM((PAIRS, columns, 2 * LANES), BF16),
         ],
         name="field",
         compiler_params=LIMIT,
     )(resident(noise), resident(received), resident(kappa_split), resident(norm_split), vert_factor)
-    profiles = lax.all_to_all(answers, "tile", split_axis=0, concat_axis=0, tiled=True)
-
+    gathered = lax.all_to_all(answers, **exchange)
     perturbation = pl.pallas_call(
         weave_kernel,
         out_shape=jax.ShapeDtypeStruct((depth, tile_rows, columns), BF16),
@@ -340,7 +407,21 @@
         name="weave",
         compiler_params=LIMIT,
     )(resident(field))
-    return (perturbation, profiles[None])
+    chunks = levels // (2 * SUB)
+    profiles = pl.pallas_call(
+        lambda *refs: unpack_kernel(order, *refs),
+        out_shape=jax.ShapeDtypeStruct((depth, tiles, slots), BF16),
+        in_specs=[VMEM],
+        out_specs=pl.BlockSpec(memory_space=pl.ANY),
+        scratch_shapes=[
+            pltpu.VMEM((levels, tiles, slots), F32),
+            pltpu.VMEM((levels, tiles, slots), BF16),
+            pltpu.SemaphoreType.DMA((chunks,)),
+        ],
+        name="unpack",
+        compiler_params=LIMIT,
+    )(resident(gathered))
+    return (perturbation, jnp.transpose(profiles, (1, 0, 2))[None])
 
 
 def solution(mesh):

time: 40.6 us -> 33.3 us (0.82); the launches traced: 39.8 us -> 32.9 us
  waiting for transfers between devices: 13.3 us -> 7.56 us
  Pallas kernels: 12.5 us -> 11 us
  starting transfers between devices: 11.9 us -> 13 us
  local copies, waits for them, and re-layouts: 1.46 us -> 0.66 us
    all_to_all x2, waiting for transfers between devices: 13.3 us -> 7.56 us  [the longest x1 6.7 us: body(): gathered = lax.all_to_all(answers, **exchange)]
    pallas_call x1, Pallas kernels: 7.49 us -> 5.03 us  [body(): pl.pallas_call(lambda *refs: field_kernel(tiles, *refs), out_shape=(jax.S...]
    all_to_all x2, starting transfers between devices: 11.9 us -> 13 us  [the longest x1 7.58 us: body(): received = lax.all_to_all(packed, **exchange)]
    pallas_call x0 -> x1, Pallas kernels: none -> 1.04 us  [body(): pl.pallas_call(lambda *refs: unpack_kernel(order, *refs), out_shape=jax.S...]
    unnamed x9 -> x8, local copies, waits for them, and re-layouts: 1.46 us -> 0.66 us
  transfers between devices with their start and end apart: 2 -> 2, of which waited for: 2 -> 2; matrix products, arithmetic and copies ran while one was open for 0% -> 0% of each run, Pallas kernels for 8% -> 10%
where the time goes in v4:
time: 33.3 us; the launch traced here: 32.9 us
  starting transfers between devices  13 us (39%)
  Pallas kernels  11 us (33%)
  waiting for transfers between devices  7.56 us (23%)
  local copies, waits for them, and re-layouts  0.66 us (2%)
  between operations  0.66 us (2%)
    all_to_all x1, starting transfers between devices, body(): received = lax.all_to_all(packed, **exchange)  7.58 us
    all_to_all x1, waiting for transfers between devices, body(): gathered = lax.all_to_all(answers, **exchange)  6.7 us
    all_to_all x1, starting transfers between devices, body(): gathered = lax.all_to_all(answers, **exchange)  5.46 us
    pallas_call x1, Pallas kernels, body(): pl.pallas_call(lambda *refs: field_kernel(tiles, *refs), out_shape=(jax.S...  5.03 us
    pallas_call x1, Pallas kernels, body(): pl.pallas_call(lambda *refs: noise_kernel(total_rows, tile_rows, columns,...  2.13 us
    pallas_call x1, Pallas kernels, body(): pl.pallas_call(pack_kernel, out_shape=(jax.ShapeDtypeStruct((tiles, parts...  1.71 us
    pallas_call x1, Pallas kernels, body(): pl.pallas_call(weave_kernel, out_shape=jax.ShapeDtypeStruct((depth, tile_...  1.1 us
    pallas_call x1, Pallas kernels, body(): pl.pallas_call(lambda *refs: unpack_kernel(order, *refs), out_shape=jax.S...  1.04 us
  transfers between devices with their start and end apart: 2, of which 2 were waited for; matrix products, arithmetic and copies ran while one was open for 0% of the time, Pallas kernels for 10%

profile of v4, /device:TPU:1, one launch (start us, length us, event | category | flops | bytes accessed | tf_op | source)
XLA Modules:
  0.0 32.9 jit_solution(420101942488957122)
XLA Ops:
  0.6 0.0 copy-start
  0.6 1.7 %pack.1 = (bf16[16,24,128]{2,1,0:T(8,128)(2,1)}, f32[8,256]{1,0:T(8,128)}, f32[8,256]{1,0:T(8,128)}) custom-call(f32[8,256]{1,0:T(8,128)} %diff_ref.1, s32[8,256]{1,0:T(8,128)} %wet_ref.1, f32[8,256]{1,0:T(8,128)} %norm_ref.1, s32[16,128]{1,0:T(8,128)} %bitcast.7, f32[16,2,128]{2,1,0:T(2,128)} %bitcast.6, s32[1,16]{1,0:T(1,128)} %count_ref.1), custom_call_target="tpu_custom_call" | custom-call | tf_op jit(solution)/shard_map/pack/pallas_call | solution.py:353
  2.4 0.0 copy-start.1
  2.4 0.0 copy-start.2
  2.4 7.6 %all-to-all-start = ((bf16[16,24,128]{2,1,0:T(8,128)(2,1)}), bf16[16,24,128]{2,1,0:T(8,128)(2,1)S(1)}, u32[]{:S(2)}, u32[]{:S(2)}) async-start(bf16[16,24,128]{2,1,0:T(8,128)(2,1)} %get-tuple-element.7), calls=%async_computation | async-start | bytes 196608 | tf_op jit(solution)/shard_map/all_to_all | solution.py:368
  9.9 0.0 copy-start.3
  9.9 0.6 %copy-done.3 = s32[2]{0:T(128)S(1)} copy-done((s32[2]{0:T(128)S(1)}, s32[2]{0:T(128)}, u32[]{:S(2)}) %copy-start.3) | copy-done | bytes 32
  10.6 2.1 %noise.1.refs_0_ = f32[100,40,128]{2,1,0:T(8,128)S(1)} custom-call(s32[2]{0:T(128)S(1)} %copy-done.3), custom_call_target="tpu_custom_call" | custom-call | tf_op jit(solution)/shard_map/noise/pallas_call | solution.py:370
  12.7 0.9 %all-to-all-done.refs_1_ = bf16[16,24,128]{2,1,0:T(8,128)(2,1)S(1)} async-done(((bf16[16,24,128]{2,1,0:T(8,128)(2,1)}), bf16[16,24,128]{2,1,0:T(8,128)(2,1)S(1)}, u32[]{:S(2)}, u32[]{:S(2)}) %all-to-all-start) | async-done | bytes 98336 | tf_op jit(solution)/shard_map/all_to_all | solution.py:368
  13.6 0.0 copy-done
  13.6 0.0 copy-done.1
  13.6 0.0 copy-done.2
  13.6 5.0 %field.1 = (bf16[16,75,128]{2,1,0:T(8,128)(2,1)}, bf16[720,256]{1,0:T(8,128)(2,1)S(1)}) custom-call(f32[100,40,128]{2,1,0:T(8,128)S(1)} %noise.1.refs_0_, bf16[16,24,128]{2,1,0:T(8,128)(2,1)S(1)} %all-to-all-done.refs_1_, f32[8,256]{1,0:T(8,128)S(1)} %copy-done.1, f32[8,256]{1,0:T(8,128)S(1)} %copy-done.2, f32[75,75]{1,0:T(8,128)S(1)} %copy-done), custom_call_target="tpu_custom_call" | custom-call | tf_op jit(solution)/shard_map/field/pallas_call | solution.py:380
  18.6 5.5 %all-to-all-start.1 = ((bf16[16,75,128]{2,1,0:T(8,128)(2,1)}), bf16[16,75,128]{2,1,0:T(8,128)(2,1)S(1)}, u32[]{:S(2)}, u32[]{:S(2)}) async-start(bf16[16,75,128]{2,1,0:T(8,128)(2,1)} %get-tuple-element.11), calls=%async_computation.1 | async-start | bytes 655360 | tf_op jit(solution)/shard_map/all_to_all | solution.py:400
  24.1 1.1 %weave.1 = bf16[75,8,256]{2,1,0:T(8,128)(2,1)} custom-call(bf16[720,256]{1,0:T(8,128)(2,1)S(1)} %get-tuple-element.10.field_ref), custom_call_target="tpu_custom_call" | custom-call | tf_op jit(solution)/shard_map/weave/pallas_call | solution.py:401
  25.2 6.7 %all-to-all-done.1.refs_0_ = bf16[16,75,128]{2,1,0:T(8,128)(2,1)S(1)} async-done(((bf16[16,75,128]{2,1,0:T(8,128)(2,1)}), bf16[16,75,128]{2,1,0:T(8,128)(2,1)S(1)}, u32[]{:S(2)}, u32[]{:S(2)}) %all-to-all-start.1) | async-done | bytes 307232 | tf_op jit(solution)/shard_map/all_to_all | solution.py:400
  31.9 1.0 %unpack.1 = bf16[75,16,128]{2,1,0:T(8,128)(2,1)} custom-call(bf16[16,75,128]{2,1,0:T(8,128)(2,1)S(1)} %all-to-all-done.1.refs_0_), custom_call_target="tpu_custom_call" | custom-call | tf_op jit(solution)/shard_map/unpack/pallas_call | solution.py:411
Async XLA Ops:
  0.6 13.0 %copy-start = (f32[75,75]{1,0:T(8,128)S(1)}, f32[75,75]{1,0:T(8,128)}, u32[]{:S(2)}) copy-start(f32[75,75]{1,0:T(8,128)} %refs_4_.1) | copy-start | bytes 67504
  2.4 11.2 %copy-start.1 = (f32[8,256]{1,0:T(8,128)S(1)}, f32[8,256]{1,0:T(8,128)}, u32[]{:S(2)}) copy-start(f32[8,256]{1,0:T(8,128)} %get-tuple-element.8.refs_2_) | copy-start | bytes 24580
  2.4 11.2 %copy-start.2 = (f32[8,256]{1,0:T(8,128)S(1)}, f32[8,256]{1,0:T(8,128)}, u32[]{:S(2)}) copy-start(f32[8,256]{1,0:T(8,128)} %get-tuple-element.9.refs_3_) | copy-start | bytes 24580
  2.4 11.2 %all-to-all-start = ((bf16[16,24,128]{2,1,0:T(8,128)(2,1)}), bf16[16,24,128]{2,1,0:T(8,128)(2,1)S(1)}, u32[]{:S(2)}, u32[]{:S(2)}) async-start(bf16[16,24,128]{2,1,0:T(8,128)(2,1)} %get-tuple-element.7), calls=%async_computation | async-start | bytes 196608 | tf_op jit(solution)/shard_map/all_to_all | solution.py:368
  9.9 0.7 %copy-start.3 = (s32[2]{0:T(128)S(1)}, s32[2]{0:T(128)}, u32[]{:S(2)}) copy-start(s32[2]{0:T(128)} %refs_0_.1) | copy-start | bytes 28
  18.6 13.3 %all-to-all-start.1 = ((bf16[16,75,128]{2,1,0:T(8,128)(2,1)}), bf16[16,75,128]{2,1,0:T(8,128)(2,1)S(1)}, u32[]{:S(2)}, u32[]{:S(2)}) async-start(bf16[16,75,128]{2,1,0:T(8,128)(2,1)} %get-tuple-element.11), calls=%async_computation.1 | async-start | bytes 655360 | tf_op jit(solution)/shard_map/all_to_all | solution.py:400

commit v5 on v4

--- a/solution.py
+++ b/solution.py
@@ -14,16 +14,23 @@
 WAYS = 4
 TOGETHER = 5
 PAIRS = 8
+SENT = 2
+QUAD = 4
 I32 = jnp.int32
 GOLDEN = -1640531535
 ROOT12 = 3.4641016151377544
 VMEM = pl.BlockSpec(memory_space=pltpu.VMEM)
 SMEM = pl.BlockSpec(memory_space=pltpu.SMEM)
+ANY = pl.BlockSpec(memory_space=pl.ANY)
 LIMIT = pltpu.CompilerParams(vmem_limit_bytes=24 << 20)
 
 
 def resident(array):
     return pltpu.with_memory_space_constraint(array, pltpu.VMEM)
+
+
+def distant(array):
+    return pltpu.with_memory_space_constraint(array, pltpu.HBM)
 
 
 def up(value, unit):
@@ -104,8 +111,62 @@
     return hashed
 
 
-def noise_kernel(total_rows, tile_rows, columns, seed_ref, out_ref):
+def spread(ref, k, row):
+    return ref[k, pl.ds(row, SUB, stride=0), :]
+
+
+def couple(root, rows, root_ref, keep_ref, gain_ref):
+    run = root.shape[1] // WAYS
+    groups = LANES // run
+    lane = iota((1, LANES), 1)
+    roots = []
+    for k in range(WAYS):
+        vector = root[:, (k // groups) * LANES : (k // groups + 1) * LANES]
+        turned = pltpu.roll(vector, run, 1)
+        keeps = (lane >= run) if k % groups else (lane < run)
+        roots.append(jnp.where(keeps, vector, turned))
+        root_ref[k] = roots[k]
+    low, high = (lane == 0) | (lane == run), (lane == run - 1) | (lane == LANES - 1)
+    inner = slice(1, rows - 1)
+    west = [jnp.where(low, 0.0, pltpu.roll(roots[-1], 1, 1))] + roots[:-1]
+    east = roots[1:] + [jnp.where(high, 0.0, pltpu.roll(roots[0], LANES - 1, 1))]
+    for k in range(WAYS):
+        near = root_ref[k, : rows - 2] + root_ref[k, 2:rows] + (west[k] + east[k])[inner]
+        keep_ref[k, inner] = 1.0 - roots[k][inner] * near
+        gain_ref[k, inner] = roots[k][inner] * roots[k][inner]
+
+
+def step_on(above, here, under, keep, gain, run):
+    lanes = iota((SUB, LANES), 1)
+    low, high = (lanes == 0) | (lanes == run), (lanes == run - 1) | (lanes == LANES - 1)
+    west = [jnp.where(low, 0.0, pltpu.roll(here[-1], 1, 1))] + here[:-1]
+    east = here[1:] + [jnp.where(high, 0.0, pltpu.roll(here[0], LANES - 1, 1))]
+    return [
+        keep[k] * here[k] + gain[k] * ((above[k] + under[k]) + (west[k] + east[k]))
+        for k in range(WAYS)
+    ]
+
+
+def early_rows(tile_rows):
+    steps = range(1, min(STEPS, (tile_rows - 1) // 2) + 1)
+    return [(step, row) for step in steps for row in range(step, tile_rows - step)]
+
+
+def noise_kernel(
+    total_rows, tile_rows, columns, seed_ref, kappa_ref, norm_ref, vert_ref,
+    out_ref, early_ref, kappa_out, norm_out, factor_ref, root_ref, keep_ref, gain_ref, vert_pad,
+):
+    kappa_out[...] = kappa_ref[...]
+    norm_out[...] = norm_ref[...]
+    depth, levels = vert_ref.shape[0], factor_ref.shape[0]
+    vert_pad[...] = jnp.zeros_like(vert_pad)
+    vert_pad[:depth, :depth] = vert_ref[...]
+    vert = vert_pad[...]
+    head = vert.astype(BF16).astype(F32)
+    factor = head + pltpu.roll(head, levels, 1) + pltpu.roll(vert - head, 2 * levels, 1)
+    factor_ref[...] = factor.astype(BF16)[:, : 3 * levels]
     planes, height, _ = out_ref.shape
+    couple(jnp.sqrt(kappa_ref[...]), tile_rows, root_ref, keep_ref, gain_ref)
     run = columns // WAYS
     groups = LANES // run
     first_row = lax.axis_index("tile") * tile_rows - STEPS
@@ -122,19 +183,34 @@
     def one_tile(part, carry):
         start = origin + part * wrapped(groups * SUB * step_level)
         span = pl.ds(pl.multiple_of(part * SUB, SUB), SUB)
+        known = {}
         for plane in range(planes):
             offset = start + wrapped(((plane // WAYS) * columns + plane % WAYS) * GOLDEN)
             hashed = mix(mix(base + offset) ^ second)
             drawn = lax.shift_right_logical(hashed, 8).astype(F32)
-            out_ref[plane, span, :] = drawn * gain + shift
+            drawn = drawn * gain + shift
+            row = plane // WAYS - STEPS
+            if 0 <= row < tile_rows:
+                drawn = drawn * spread(root_ref, plane % WAYS, row)
+                known.setdefault((0, row), []).append(drawn)
+            out_ref[plane, span, :] = drawn
+        for place, (step, row) in enumerate(early_rows(tile_rows)):
+            known[step, row] = step_on(
+                known[step - 1, row - 1], known[step - 1, row], known[step - 1, row + 1],
+                [spread(keep_ref, k, row) for k in range(WAYS)],
+                [spread(gain_ref, k, row) for k in range(WAYS)],
+                run,
+            )
+            for k in range(WAYS):
+                early_ref[WAYS * place + k, span, :] = known[step, row][k]
         return carry
 
     lax.fori_loop(0, height // SUB, one_tile, 0)
 
 
 def field_kernel(
-    tiles, noise_ref, recv_ref, kappa_ref, norm_ref, vert_ref, prof_ref, field_ref,
-    halo_ref, root_ref, keep_ref, gain_ref, vert_pad, state_ref, hat_ref,
+    tiles, noise_ref, early_ref, recv_ref, kappa_ref, norm_ref, factor_ref, prof_hbm, field_ref,
+    halo_ref, root_ref, keep_ref, gain_ref, state_ref, hat_ref, prof_ref, sems,
 ):
     planes, height, _ = noise_ref.shape
     rows = planes // WAYS
@@ -142,7 +218,7 @@
     run = columns // WAYS
     groups = LANES // run
     levels = height * groups
-    depth = vert_ref.shape[0]
+    depth = QUAD * prof_ref.shape[1]
     out_rows = tile_rows + 1
     parts = columns // LANES
     tile = lax.axis_index("tile")
@@ -158,26 +234,7 @@
                 given[k * tile_rows : k * tile_rows + count]
             )
     root = jnp.sqrt(halo_ref[...])
-    lane = iota((1, LANES), 1)
-    roots = []
-    for k in range(WAYS):
-        vector = root[:, (k // groups) * LANES : (k // groups + 1) * LANES]
-        turned = pltpu.roll(vector, run, 1)
-        keeps = (lane >= run) if k % groups else (lane < run)
-        roots.append(jnp.where(keeps, vector, turned))
-        root_ref[k] = roots[k]
-    edge_low, edge_high = (lane == 0) | (lane == run), (lane == run - 1) | (lane == LANES - 1)
-    inner = slice(1, rows - 1)
-    for k in range(WAYS):
-        west = roots[k - 1] if k else jnp.where(edge_low, 0.0, pltpu.roll(roots[-1], 1, 1))
-        east = (
-            roots[k + 1]
-            if k < WAYS - 1
-            else jnp.where(edge_high, 0.0, pltpu.roll(roots[0], LANES - 1, 1))
-        )
-        near = root_ref[k, : rows - 2] + root_ref[k, 2:rows] + (west + east)[inner]
-        keep_ref[k, inner] = 1.0 - roots[k][inner] * near
-        gain_ref[k, inner] = roots[k][inner] * roots[k][inner]
+    couple(root, rows, root_ref, keep_ref, gain_ref)
     kappa = halo_ref[STEPS : STEPS + out_rows]
     wet = kappa > 0.0
     inverse = jnp.where(wet, root[STEPS : STEPS + out_rows] / jnp.where(wet, kappa, 1.0), 0.0)
@@ -185,13 +242,7 @@
     norm_below = jnp.concatenate([below[k : k + 1] for k in range(parts)], 1)
     scales = inverse * jnp.concatenate([norm_ref[...], norm_below], 0)
 
-    block = (SUB, LANES)
-    lanes = iota(block, 1)
-    low8, high8 = (lanes == 0) | (lanes == run), (lanes == run - 1) | (lanes == LANES - 1)
-    lower = lanes < run
-
-    def spread(ref, k, row):
-        return ref[k, pl.ds(row, SUB, stride=0), :]
+    lower = iota((SUB, LANES), 1) < run
 
     def diffuse(bundle, carry):
         spans = [
@@ -199,31 +250,29 @@
         ]
         known = [{} for _ in range(STEPS + 1)]
 
+        own = range(STEPS, STEPS + tile_rows)
+
         def drawn(row):
-            cells = []
-            for k in range(WAYS):
-                scale = spread(root_ref, k, row)
-                cells.append([noise_ref[WAYS * row + k, span, :] * scale for span in spans])
+            cells = [[noise_ref[WAYS * row + k, span, :] for span in spans] for k in range(WAYS)]
+            if row not in own:
+                scales = [spread(root_ref, k, row) for k in range(WAYS)]
+                cells = [[cell * scales[k] for cell in cells[k]] for k in range(WAYS)]
             return cells
 
-        def stepped(past, row):
-            here, fresh = past[row], []
-            for k in range(WAYS):
-                keep, gain = spread(keep_ref, k, row), spread(gain_ref, k, row)
-                cells = []
-                for part in range(TOGETHER):
-                    if k:
-                        west = here[k - 1][part]
-                    else:
-                        west = jnp.where(low8, 0.0, pltpu.roll(here[-1][part], 1, 1))
-                    if k < WAYS - 1:
-                        east = here[k + 1][part]
-                    else:
-                        east = jnp.where(high8, 0.0, pltpu.roll(here[0][part], LANES - 1, 1))
-                    near = (past[row - 1][k][part] + past[row + 1][k][part]) + (west + east)
-                    cells.append(keep * here[k][part] + gain * near)
-                fresh.append(cells)
-            return fresh
+        def stepped(step, row):
+            if (step, row - STEPS) in early_rows(tile_rows):
+                first = WAYS * early_rows(tile_rows).index((step, row - STEPS))
+                return [[early_ref[first + k, span, :] for span in spans] for k in range(WAYS)]
+            past = known[step - 1]
+            keep = [spread(keep_ref, k, row) for k in range(WAYS)]
+            gain = [spread(gain_ref, k, row) for k in range(WAYS)]
+            fresh = [
+                step_on(*([cells[k][part] for k in range(WAYS)] for cells in (
+                    past[row - 1], past[row], past[row + 1]
+                )), keep, gain, run)
+                for part in range(TOGETHER)
+            ]
+            return [[fresh[part][k] for part in range(TOGETHER)] for k in range(WAYS)]
 
         for top in range(rows):
             known[0][top] = drawn(top)
@@ -231,7 +280,7 @@
                 row = top - step
                 if row < step:
                     break
-                known[step][row] = stepped(known[step - 1], row)
+                known[step][row] = stepped(step, row)
                 del known[step - 1][row - 1]
         for row in range(out_rows):
             done = known[STEPS][row + STEPS]
@@ -252,16 +301,10 @@
 
     lax.fori_loop(0, height // SUB // TOGETHER, diffuse, 0)
 
-    vert_pad[...] = jnp.zeros_like(vert_pad)
-    vert_pad[:depth, :depth] = vert_ref[...]
-    vert = vert_pad[...]
-    head = vert.astype(BF16).astype(F32)
-    factor = head + pltpu.roll(head, levels, 1) + pltpu.roll(vert - head, 2 * levels, 1)
-    factor = factor.astype(BF16)[:, : 3 * levels]
     bunch = 2 * SUB
     for row in range(out_rows):
         mixed = jnp.dot(
-            factor,
+            factor_ref[...],
             state_ref[:, row * columns : (row + 1) * columns],
             preferred_element_type=F32,
         )
@@ -270,19 +313,24 @@
             first = (part * out_rows + row) * bunch
             field_ref[first : first + bunch, :] = scaled[part * bunch : (part + 1) * bunch]
 
-    col = column_of(iota((columns, 2 * LANES), 0), columns).astype(F32)
+    col = column_of(iota((columns, 2 * LANES), 0), columns).astype(BF16)
 
     def positions(pair, first):
         tails = [recv_ref[2 * pair + k, parts * tile_rows :, :].astype(F32) for k in range(2)]
         tail = jnp.concatenate(tails, 1)
-        return tail[first : first + 1] + (tail[first + 1 : first + 2] + tail[first + 2 : first + 3])
+        return tail[first : first + 1], tail[first + 1 : first + 2] + tail[first + 2 : first + 3]
 
     def make_hat(pair, slot):
-        hat_ref[slot] = jnp.maximum(1.0 - jnp.abs(positions(pair, parts) - col), 0.0).astype(BF16)
+        near, frac_x = positions(pair, parts)
+        hat_ref[slot] = jnp.where(
+            col == near.astype(BF16),
+            (1.0 - frac_x).astype(BF16),
+            jnp.where(col == (near + 1.0).astype(BF16), frac_x.astype(BF16), jnp.zeros_like(col)),
+        )
 
     def answer(pair, hat):
         along = jnp.dot(field_ref[...], hat, preferred_element_type=F32)
-        pos_y = positions(pair, parts + 3)
+        pos_y = sum(positions(pair, parts + 3))
         weights = [jnp.maximum(1.0 - jnp.abs(pos_y - float(row)), 0.0) for row in range(out_rows)]
         for part in range(levels // bunch):
             total = None
@@ -290,19 +338,29 @@
                 first = (part * out_rows + row) * bunch
                 term = along[first : first + bunch] * weights[row]
                 total = term if total is None else total + term
-            kept = min(bunch, depth - part * bunch)
-            rounded = total.astype(BF16)[:kept]
-            prof_ref[2 * pair, part * bunch : part * bunch + kept, :] = rounded[:, :LANES]
-            prof_ref[2 * pair + 1, part * bunch : part * bunch + kept, :] = rounded[:, LANES:]
+            kept = min(bunch // QUAD, -(-(depth - part * bunch) // QUAD))
+            at = slice(part * bunch // QUAD, part * bunch // QUAD + kept)
+            rounded = total.astype(BF16)[: kept * QUAD]
+            for half in range(2):
+                lanes = slice(half * LANES, (half + 1) * LANES)
+                prof_ref[2 * pair + half, at] = rounded[:, lanes].reshape(kept, QUAD, LANES)
 
     def some_pairs(step, carry):
         for slot in range(PAIRS):
             make_hat(step * PAIRS + slot, slot)
         for slot in range(PAIRS):
             answer(step * PAIRS + slot, hat_ref[slot])
+            if (slot + 1) % SENT == 0:
+                sending((step * PAIRS + slot + 1) // SENT - 1).start()
         return carry
 
+    def sending(batch):
+        at = pl.ds(batch * 2 * SENT, 2 * SENT)
+        return pltpu.make_async_copy(prof_ref.at[at], prof_hbm.at[at], sems.at[batch])
+
     lax.fori_loop(0, tiles // (2 * PAIRS), some_pairs, 0)
+    for batch in range(tiles // (2 * SENT)):
+        sending(batch).wait()
 
 
 def weave_kernel(field_ref, out_ref, flat_ref):
@@ -320,13 +378,15 @@
 
 
 def unpack_kernel(order, given_ref, out_ref, wide_ref, ready_ref, sems):
-    depth = given_ref.shape[1]
+    depth = out_ref.shape[0]
     bunch = 2 * SUB
     copies = []
     for part, start in enumerate(range(0, depth, bunch)):
         stop = min(start + bunch, depth)
         for place, owner in enumerate(order):
-            wide_ref[start:stop, owner, :] = given_ref[place, start:stop, :].astype(F32)
+            quads = given_ref[place, start // QUAD : -(-stop // QUAD)]
+            rows = quads.reshape(quads.shape[0] * QUAD, LANES)
+            wide_ref[start : start + rows.shape[0], owner, :] = rows.astype(F32)
         ready_ref[start:stop] = wide_ref[start:stop].astype(BF16)
         copies.append(
             pltpu.make_async_copy(ready_ref.at[start:stop], out_ref.at[start:stop], sems.at[part])
@@ -367,36 +427,48 @@
     )
     received = lax.all_to_all(packed, **exchange)
 
-    noise = pl.pallas_call(
+    own = pltpu.VMEM((WAYS, up(tile_rows, SUB), LANES), F32)
+    early = len(early_rows(tile_rows))
+    noise, ahead, *settled = pl.pallas_call(
         lambda *refs: noise_kernel(total_rows, tile_rows, columns, *refs),
-        out_shape=pltpu.VMEM((WAYS * rows, levels // groups, LANES), F32),
-        in_specs=[SMEM],
-        out_specs=VMEM,
+        out_shape=(
+            pltpu.VMEM((WAYS * rows, levels // groups, LANES), F32),
+            pltpu.VMEM((WAYS * early, levels // groups, LANES), F32),
+            pltpu.VMEM(diffusivity.shape, F32),
+            pltpu.VMEM(diffusivity.shape, F32),
+            pltpu.VMEM((levels, 3 * levels), BF16),
+        ),
+        in_specs=[SMEM, VMEM, VMEM, VMEM],
+        out_specs=(VMEM,) * 5,
+        scratch_shapes=[own, own, own, pltpu.VMEM((levels, up(3 * levels, LANES)), F32)],
         name="noise",
         compiler_params=LIMIT,
-    )(noise_seeds)
+    )(*(distant(part) for part in (noise_seeds, kappa_split, norm_split, vert_factor)))
 
     coefficients = pltpu.VMEM((WAYS, up(rows, SUB), LANES), F32)
     answers, field = pl.pallas_call(
         lambda *refs: field_kernel(tiles, *refs),
         out_shape=(
-            jax.ShapeDtypeStruct((tiles, depth, slots), BF16),
+            pltpu.HBM((tiles, up(depth, QUAD) // QUAD, QUAD, slots), BF16),
             pltpu.VMEM(((tile_rows + 1) * levels, columns), BF16),
         ),
-        in_specs=[VMEM] * 5,
-        out_specs=(VMEM, VMEM),
+        in_specs=[VMEM] * 6,
+        out_specs=(ANY, VMEM),
         scratch_shapes=[
             pltpu.VMEM((up(rows, SUB), columns), F32),
             coefficients,
             coefficients,
             coefficients,
-            pltpu.VMEM((levels, up(3 * levels, LANES)), F32),
             pltpu.VMEM((3 * levels, (tile_rows + 1) * columns), BF16),
             pltpu.VMEM((PAIRS, columns, 2 * LANES), BF16),
+            pltpu.VMEM((tiles, up(depth, QUAD) // QUAD, QUAD, slots), BF16),
+            pltpu.SemaphoreType.DMA((tiles // (2 * SENT),)),
         ],
         name="field",
         compiler_params=LIMIT,
-    )(resident(noise), resident(received), resident(kappa_split), resident(norm_split), vert_factor)
+    )(
+        *(resident(part) for part in (noise, ahead, received, *settled))
+    )
     gathered = lax.all_to_all(answers, **exchange)
     perturbation = pl.pallas_call(
         weave_kernel,
@@ -412,7 +484,7 @@
         lambda *refs: unpack_kernel(order, *refs),
         out_shape=jax.ShapeDtypeStruct((depth, tiles, slots), BF16),
         in_specs=[VMEM],
-        out_specs=pl.BlockSpec(memory_space=pl.ANY),
+        out_specs=ANY,
         scratch_shapes=[
             pltpu.VMEM((levels, tiles, slots), F32),
             pltpu.VMEM((levels, tiles, slots), BF16),

time: 33.3 us -> 32.6 us (0.979)
  local copies, waits for them, and re-layouts: 0.66 us -> 0 us
  Pallas kernels: 11 us -> 11.6 us
  waiting for transfers between devices: 7.56 us -> 7.06 us
    pallas_call x1, Pallas kernels: 2.13 us -> 2.96 us  [body(): pl.pallas_call(lambda *refs: noise_kernel(total_rows, tile_rows, columns,...]
    unnamed x8 -> x0, local copies, waits for them, and re-layouts: 0.66 us -> none
  transfers between devices with their start and end apart: 2 -> 2, of which waited for: 2 -> 2; matrix products, arithmetic and copies ran while one was open for 0% -> 0% of each run, Pallas kernels for 10% -> 13%
where the time goes in v5:
time: 32.6 us; the launch traced here: 32.2 us
  starting transfers between devices  12.9 us (40%)
  Pallas kernels  11.6 us (36%)
  waiting for transfers between devices  7.06 us (22%)
  between operations  0.65 us (2%)
    all_to_all x1, starting transfers between devices, body(): received = lax.all_to_all(packed, **exchange)  7.44 us
    all_to_all x1, waiting for transfers between devices, body(): gathered = lax.all_to_all(answers, **exchange)  6.37 us
    all_to_all x1, starting transfers between devices, body(): gathered = lax.all_to_all(answers, **exchange)  5.47 us
    pallas_call x1, Pallas kernels, body(): pl.pallas_call(lambda *refs: field_kernel(tiles, *refs), out_shape=(pltpu...  4.76 us
    pallas_call x1, Pallas kernels, body(): pl.pallas_call(lambda *refs: noise_kernel(total_rows, tile_rows, columns,...  2.96 us
    pallas_call x1, Pallas kernels, body(): pl.pallas_call(pack_kernel, out_shape=(jax.ShapeDtypeStruct((tiles, parts...  1.71 us
    pallas_call x1, Pallas kernels, body(): pl.pallas_call(weave_kernel, out_shape=jax.ShapeDtypeStruct((depth, tile_...  1.1 us
    pallas_call x1, Pallas kernels, body(): pl.pallas_call(lambda *refs: unpack_kernel(order, *refs), out_shape=jax.S...  1.08 us
  transfers between devices with their start and end apart: 2, of which 2 were waited for; matrix products, arithmetic and copies ran while one was open for 0% of the time, Pallas kernels for 13%

profile of v5, /device:TPU:1, one launch (start us, length us, event | category | flops | bytes accessed | tf_op | source)
XLA Modules:
  0.0 32.2 jit_solution(38414650348217717)
XLA Ops:
  0.6 1.7 %pack.1 = (bf16[16,24,128]{2,1,0:T(8,128)(2,1)}, f32[8,256]{1,0:T(8,128)}, f32[8,256]{1,0:T(8,128)}) custom-call(f32[8,256]{1,0:T(8,128)} %diff_ref.1, s32[8,256]{1,0:T(8,128)} %wet_ref.1, f32[8,256]{1,0:T(8,128)} %norm_ref.1, s32[16,128]{1,0:T(8,128)} %bitcast.7, f32[16,2,128]{2,1,0:T(2,128)} %bitcast.6, s32[1,16]{1,0:T(1,128)} %count_ref.1), custom_call_target="tpu_custom_call" | custom-call | tf_op jit(solution)/shard_map/pack/pallas_call | solution.py:413
  2.3 7.4 %all-to-all-start = ((bf16[16,24,128]{2,1,0:T(8,128)(2,1)}), bf16[16,24,128]{2,1,0:T(8,128)(2,1)S(1)}, u32[]{:S(2)}, u32[]{:S(2)}) async-start(bf16[16,24,128]{2,1,0:T(8,128)(2,1)} %get-tuple-element.16), calls=%async_computation | async-start | bytes 196608 | tf_op jit(solution)/shard_map/all_to_all | solution.py:428
  9.8 3.0 %noise.1 = (f32[100,40,128]{2,1,0:T(8,128)S(1)}, f32[48,40,128]{2,1,0:T(8,128)S(1)}, f32[8,256]{1,0:T(8,128)S(1)}, f32[8,256]{1,0:T(8,128)S(1)}, bf16[80,240]{1,0:T(8,128)(2,1)S(1)}) custom-call(s32[2]{0:T(128)} %refs_0_.1, f32[8,256]{1,0:T(8,128)} %get-tuple-element.12.refs_1_, f32[8,256]{1,0:T(8,128)} %get-tuple-element.13.refs_2_, f32[75,75]{1,0:T(8,128)} %refs_3_.1), custom_call_target="tpu_custom_call" | custom-call | tf_op jit(solution)/shard_map/noise/pallas_call | solution.py:432
  12.7 0.7 %all-to-all-done.refs_2_ = bf16[16,24,128]{2,1,0:T(8,128)(2,1)S(1)} async-done(((bf16[16,24,128]{2,1,0:T(8,128)(2,1)}), bf16[16,24,128]{2,1,0:T(8,128)(2,1)S(1)}, u32[]{:S(2)}, u32[]{:S(2)}) %all-to-all-start) | async-done | bytes 98336 | tf_op jit(solution)/shard_map/all_to_all | solution.py:428
  13.4 4.8 %field.1 = (bf16[16,19,4,128]{3,2,1,0:T(4,128)(2,1)}, bf16[720,256]{1,0:T(8,128)(2,1)S(1)}) custom-call(f32[100,40,128]{2,1,0:T(8,128)S(1)} %get-tuple-element.14.refs_0_, f32[48,40,128]{2,1,0:T(8,128)S(1)} %get-tuple-element.15.refs_1_, bf16[16,24,128]{2,1,0:T(8,128)(2,1)S(1)} %all-to-all-done.refs_2_, f32[8,256]{1,0:T(8,128)S(1)} %get-tuple-element.17.refs_3_, ...), custom_call_target="tpu_custom_call" | custom-call | tf_op jit(solution)/shard_map/field/pallas_call | solution.py:449
  18.2 5.5 %all-to-all-start.1 = ((bf16[16,19,4,128]{3,2,1,0:T(4,128)(2,1)}), bf16[16,19,4,128]{3,2,1,0:T(4,128)(2,1)S(1)}, u32[]{:S(2)}, u32[]{:S(2)}) async-start(bf16[16,19,4,128]{3,2,1,0:T(4,128)(2,1)} %get-tuple-element.21), calls=%async_computation.1 | async-start | bytes 622592 | tf_op jit(solution)/shard_map/all_to_all | solution.py:472
  23.7 1.1 %weave.1 = bf16[75,8,256]{2,1,0:T(8,128)(2,1)} custom-call(bf16[720,256]{1,0:T(8,128)(2,1)S(1)} %get-tuple-element.20.field_ref), custom_call_target="tpu_custom_call" | custom-call | tf_op jit(solution)/shard_map/weave/pallas_call | solution.py:473
  24.8 6.4 %all-to-all-done.1.refs_0_ = bf16[16,19,4,128]{3,2,1,0:T(4,128)(2,1)S(1)} async-done(((bf16[16,19,4,128]{3,2,1,0:T(4,128)(2,1)}), bf16[16,19,4,128]{3,2,1,0:T(4,128)(2,1)S(1)}, u32[]{:S(2)}, u32[]{:S(2)}) %all-to-all-start.1) | async-done | bytes 311328 | tf_op jit(solution)/shard_map/all_to_all | solution.py:472
  31.2 1.1 %unpack.1 = bf16[75,16,128]{2,1,0:T(8,128)(2,1)} custom-call(bf16[16,19,4,128]{3,2,1,0:T(4,128)(2,1)S(1)} %all-to-all-done.1.refs_0_), custom_call_target="tpu_custom_call" | custom-call | tf_op jit(solution)/shard_map/unpack/pallas_call | solution.py:483
Async XLA Ops:
  2.3 11.1 %all-to-all-start = ((bf16[16,24,128]{2,1,0:T(8,128)(2,1)}), bf16[16,24,128]{2,1,0:T(8,128)(2,1)S(1)}, u32[]{:S(2)}, u32[]{:S(2)}) async-start(bf16[16,24,128]{2,1,0:T(8,128)(2,1)} %get-tuple-element.16), calls=%async_computation | async-start | bytes 196608 | tf_op jit(solution)/shard_map/all_to_all | solution.py:428
  18.2 12.9 %all-to-all-start.1 = ((bf16[16,19,4,128]{3,2,1,0:T(4,128)(2,1)}), bf16[16,19,4,128]{3,2,1,0:T(4,128)(2,1)S(1)}, u32[]{:S(2)}, u32[]{:S(2)}) async-start(bf16[16,19,4,128]{3,2,1,0:T(4,128)(2,1)} %get-tuple-element.21), calls=%async_computation.1 | async-start | bytes 622592 | tf_op jit(solution)/shard_map/all_to_all | solution.py:472

commit v6 on v5

--- a/solution.py
+++ b/solution.py
@@ -71,7 +71,7 @@
     order = visiting_order(owners)
     kappa = diff_ref[...] * wet_ref[...].astype(F32)
     square = (columns, columns)
-    parting = (iota(square, 0) == column_of(iota(square, 1), columns)).astype(F32)
+    parting = (iota(square, 0) == column_of(iota((1, columns), 1), columns)).astype(F32)
     both = jnp.concatenate([kappa, norm_ref[...]], 0)
     parted = jnp.dot(both, parting, precision=EXACT, preferred_element_type=F32)
     kappa_out[...] = parted[:tile_rows]
@@ -125,7 +125,7 @@
         turned = pltpu.roll(vector, run, 1)
         keeps = (lane >= run) if k % groups else (lane < run)
         roots.append(jnp.where(keeps, vector, turned))
-        root_ref[k] = roots[k]
+        root_ref[k, : root.shape[0]] = roots[k]
     low, high = (lane == 0) | (lane == run), (lane == run - 1) | (lane == LANES - 1)
     inner = slice(1, rows - 1)
     west = [jnp.where(low, 0.0, pltpu.roll(roots[-1], 1, 1))] + roots[:-1]
@@ -333,11 +333,14 @@
         pos_y = sum(positions(pair, parts + 3))
         weights = [jnp.maximum(1.0 - jnp.abs(pos_y - float(row)), 0.0) for row in range(out_rows)]
         for part in range(levels // bunch):
-            total = None
+            terms = []
             for row in range(out_rows):
                 first = (part * out_rows + row) * bunch
-                term = along[first : first + bunch] * weights[row]
-                total = term if total is None else total + term
+                terms.append(along[first : first + bunch] * weights[row])
+            while len(terms) > 1:
+                paired = [one + two for one, two in zip(terms[::2], terms[1::2])]
+                terms = paired + terms[2 * len(paired) :]
+            total = terms[0]
             kept = min(bunch // QUAD, -(-(depth - part * bunch) // QUAD))
             at = slice(part * bunch // QUAD, part * bunch // QUAD + kept)
             rounded = total.astype(BF16)[: kept * QUAD]
@@ -427,7 +430,7 @@
     )
     received = lax.all_to_all(packed, **exchange)
 
-    own = pltpu.VMEM((WAYS, up(tile_rows, SUB), LANES), F32)
+    own = pltpu.VMEM((WAYS, up(tile_rows, SUB) + SUB, LANES), F32)
     early = len(early_rows(tile_rows))
     noise, ahead, *settled = pl.pallas_call(
         lambda *refs: noise_kernel(total_rows, tile_rows, columns, *refs),

time: 32.6 us -> 32.7 us (level)
  no operation moved by 1% of the time
where the time goes in v6:
time: 32.7 us; the launch traced here: 32.3 us
  starting transfers between devices  12.9 us (39%)
  Pallas kernels  11.7 us (36%)
  waiting for transfers between devices  7.06 us (22%)
  between operations  0.65 us (2%)
    all_to_all x1, starting transfers between devices, body(): received = lax.all_to_all(packed, **exchange)  7.44 us
    all_to_all x1, waiting for transfers between devices, body(): gathered = lax.all_to_all(answers, **exchange)  6.37 us
    all_to_all x1, starting transfers between devices, body(): gathered = lax.all_to_all(answers, **exchange)  5.47 us
    pallas_call x1, Pallas kernels, body(): pl.pallas_call(lambda *refs: field_kernel(tiles, *refs), out_shape=(pltpu...  4.81 us
    pallas_call x1, Pallas kernels, body(): pl.pallas_call(lambda *refs: noise_kernel(total_rows, tile_rows, columns,...  2.96 us
    pallas_call x1, Pallas kernels, body(): pl.pallas_call(pack_kernel, out_shape=(jax.ShapeDtypeStruct((tiles, parts...  1.71 us
    pallas_call x1, Pallas kernels, body(): pl.pallas_call(weave_kernel, out_shape=jax.ShapeDtypeStruct((depth, tile_...  1.1 us
    pallas_call x1, Pallas kernels, body(): pl.pallas_call(lambda *refs: unpack_kernel(order, *refs), out_shape=jax.S...  1.08 us
  transfers between devices with their start and end apart: 2, of which 2 were waited for; matrix products, arithmetic and copies ran while one was open for 0% of the time, Pallas kernels for 13%

profile of v6, /device:TPU:1, one launch (start us, length us, event | category | flops | bytes accessed | tf_op | source)
XLA Modules:
  0.0 32.3 jit_solution(10287091155703294281)
XLA Ops:
  0.6 1.7 %pack.1 = (bf16[16,24,128]{2,1,0:T(8,128)(2,1)}, f32[8,256]{1,0:T(8,128)}, f32[8,256]{1,0:T(8,128)}) custom-call(f32[8,256]{1,0:T(8,128)} %diff_ref.1, s32[8,256]{1,0:T(8,128)} %wet_ref.1, f32[8,256]{1,0:T(8,128)} %norm_ref.1, s32[16,128]{1,0:T(8,128)} %bitcast.7, f32[16,2,128]{2,1,0:T(2,128)} %bitcast.6, s32[1,16]{1,0:T(1,128)} %count_ref.1), custom_call_target="tpu_custom_call" | custom-call | tf_op jit(solution)/shard_map/pack/pallas_call | solution.py:416
  2.3 7.4 %all-to-all-start = ((bf16[16,24,128]{2,1,0:T(8,128)(2,1)}), bf16[16,24,128]{2,1,0:T(8,128)(2,1)S(1)}, u32[]{:S(2)}, u32[]{:S(2)}) async-start(bf16[16,24,128]{2,1,0:T(8,128)(2,1)} %get-tuple-element.16), calls=%async_computation | async-start | bytes 196608 | tf_op jit(solution)/shard_map/all_to_all | solution.py:431
  9.8 3.0 %noise.1 = (f32[100,40,128]{2,1,0:T(8,128)S(1)}, f32[48,40,128]{2,1,0:T(8,128)S(1)}, f32[8,256]{1,0:T(8,128)S(1)}, f32[8,256]{1,0:T(8,128)S(1)}, bf16[80,240]{1,0:T(8,128)(2,1)S(1)}) custom-call(s32[2]{0:T(128)} %refs_0_.1, f32[8,256]{1,0:T(8,128)} %get-tuple-element.12.refs_1_, f32[8,256]{1,0:T(8,128)} %get-tuple-element.13.refs_2_, f32[75,75]{1,0:T(8,128)} %refs_3_.1), custom_call_target="tpu_custom_call" | custom-call | tf_op jit(solution)/shard_map/noise/pallas_call | solution.py:435
  12.7 0.7 %all-to-all-done.refs_2_ = bf16[16,24,128]{2,1,0:T(8,128)(2,1)S(1)} async-done(((bf16[16,24,128]{2,1,0:T(8,128)(2,1)}), bf16[16,24,128]{2,1,0:T(8,128)(2,1)S(1)}, u32[]{:S(2)}, u32[]{:S(2)}) %all-to-all-start) | async-done | bytes 98336 | tf_op jit(solution)/shard_map/all_to_all | solution.py:431
  13.4 4.8 %field.1 = (bf16[16,19,4,128]{3,2,1,0:T(4,128)(2,1)}, bf16[720,256]{1,0:T(8,128)(2,1)S(1)}) custom-call(f32[100,40,128]{2,1,0:T(8,128)S(1)} %get-tuple-element.14.refs_0_, f32[48,40,128]{2,1,0:T(8,128)S(1)} %get-tuple-element.15.refs_1_, bf16[16,24,128]{2,1,0:T(8,128)(2,1)S(1)} %all-to-all-done.refs_2_, f32[8,256]{1,0:T(8,128)S(1)} %get-tuple-element.17.refs_3_, ...), custom_call_target="tpu_custom_call" | custom-call | tf_op jit(solution)/shard_map/field/pallas_call | solution.py:452
  18.3 5.5 %all-to-all-start.1 = ((bf16[16,19,4,128]{3,2,1,0:T(4,128)(2,1)}), bf16[16,19,4,128]{3,2,1,0:T(4,128)(2,1)S(1)}, u32[]{:S(2)}, u32[]{:S(2)}) async-start(bf16[16,19,4,128]{3,2,1,0:T(4,128)(2,1)} %get-tuple-element.21), calls=%async_computation.1 | async-start | bytes 622592 | tf_op jit(solution)/shard_map/all_to_all | solution.py:475
  23.7 1.1 %weave.1 = bf16[75,8,256]{2,1,0:T(8,128)(2,1)} custom-call(bf16[720,256]{1,0:T(8,128)(2,1)S(1)} %get-tuple-element.20.field_ref), custom_call_target="tpu_custom_call" | custom-call | tf_op jit(solution)/shard_map/weave/pallas_call | solution.py:476
  24.8 6.4 %all-to-all-done.1.refs_0_ = bf16[16,19,4,128]{3,2,1,0:T(4,128)(2,1)S(1)} async-done(((bf16[16,19,4,128]{3,2,1,0:T(4,128)(2,1)}), bf16[16,19,4,128]{3,2,1,0:T(4,128)(2,1)S(1)}, u32[]{:S(2)}, u32[]{:S(2)}) %all-to-all-start.1) | async-done | bytes 311328 | tf_op jit(solution)/shard_map/all_to_all | solution.py:475
  31.2 1.1 %unpack.1 = bf16[75,16,128]{2,1,0:T(8,128)(2,1)} custom-call(bf16[16,19,4,128]{3,2,1,0:T(4,128)(2,1)S(1)} %all-to-all-done.1.refs_0_), custom_call_target="tpu_custom_call" | custom-call | tf_op jit(solution)/shard_map/unpack/pallas_call | solution.py:486
Async XLA Ops:
  2.3 11.1 %all-to-all-start = ((bf16[16,24,128]{2,1,0:T(8,128)(2,1)}), bf16[16,24,128]{2,1,0:T(8,128)(2,1)S(1)}, u32[]{:S(2)}, u32[]{:S(2)}) async-start(bf16[16,24,128]{2,1,0:T(8,128)(2,1)} %get-tuple-element.16), calls=%async_computation | async-start | bytes 196608 | tf_op jit(solution)/shard_map/all_to_all | solution.py:431
  18.3 12.9 %all-to-all-start.1 = ((bf16[16,19,4,128]{3,2,1,0:T(4,128)(2,1)}), bf16[16,19,4,128]{3,2,1,0:T(4,128)(2,1)S(1)}, u32[]{:S(2)}, u32[]{:S(2)}) async-start(bf16[16,19,4,128]{3,2,1,0:T(4,128)(2,1)} %get-tuple-element.21), calls=%async_computation.1 | async-start | bytes 622592 | tf_op jit(solution)/shard_map/all_to_all | solution.py:475

commit v7 on v6

--- a/solution.py
+++ b/solution.py
@@ -366,7 +366,12 @@
         sending(batch).wait()
 
 
-def weave_kernel(field_ref, out_ref, flat_ref):
+def weave_kernel(field_ref, out_ref, swap_ref, flat_ref):
+    size = swap_ref.shape[0]
+    bunch = 2 * SUB
+    into, source = iota((size, size), 0), iota((size, size), 1)
+    high, low = lax.shift_right_logical(into, 4), into & (bunch - 1)
+    swap_ref[...] = (source == low * bunch + high).astype(BF16)
     depth, tile_rows, columns = out_ref.shape
     levels = field_ref.shape[0] // (tile_rows + 1)
     square = (columns, columns)
@@ -380,19 +385,29 @@
     out_ref[...] = flat_ref[:depth].astype(BF16)
 
 
-def unpack_kernel(order, given_ref, out_ref, wide_ref, ready_ref, sems):
-    depth = out_ref.shape[0]
+def unpack_kernel(order, given_ref, swap_ref, out_ref, ready_ref, sems):
+    depth, owners, _ = out_ref.shape
     bunch = 2 * SUB
     copies = []
+    held = QUAD * given_ref.shape[1]
     for part, start in enumerate(range(0, depth, bunch)):
-        stop = min(start + bunch, depth)
-        for place, owner in enumerate(order):
-            quads = given_ref[place, start // QUAD : -(-stop // QUAD)]
-            rows = quads.reshape(quads.shape[0] * QUAD, LANES)
-            wide_ref[start : start + rows.shape[0], owner, :] = rows.astype(F32)
-        ready_ref[start:stop] = wide_ref[start:stop].astype(BF16)
+        end = min(start + bunch, depth)
+        taken = min(start, held - bunch)
+        for first in range(0, owners, bunch):
+            rows = jnp.concatenate(
+                [
+                    given_ref[order.index(owner), taken // QUAD : (taken + bunch) // QUAD].reshape(
+                        bunch, LANES
+                    )
+                    for owner in range(first, first + bunch)
+                ],
+                0,
+            )
+            turned = jnp.dot(swap_ref[...], rows, preferred_element_type=F32).astype(BF16)
+            turned = turned.reshape(bunch, bunch, LANES)[start - taken : end - taken]
+            ready_ref[start:end, first : first + bunch, :] = turned
         copies.append(
-            pltpu.make_async_copy(ready_ref.at[start:stop], out_ref.at[start:stop], sems.at[part])
+            pltpu.make_async_copy(ready_ref.at[start:end], out_ref.at[start:end], sems.at[part])
         )
         copies[-1].start()
     for copy in copies:
@@ -473,11 +488,14 @@
         *(resident(part) for part in (noise, ahead, received, *settled))
     )
     gathered = lax.all_to_all(answers, **exchange)
-    perturbation = pl.pallas_call(
+    perturbation, swap = pl.pallas_call(
         weave_kernel,
-        out_shape=jax.ShapeDtypeStruct((depth, tile_rows, columns), BF16),
+        out_shape=(
+            jax.ShapeDtypeStruct((depth, tile_rows, columns), BF16),
+            pltpu.VMEM((4 * SUB * SUB, 4 * SUB * SUB), BF16),
+        ),
         in_specs=[VMEM],
-        out_specs=VMEM,
+        out_specs=(VMEM, VMEM),
         scratch_shapes=[pltpu.VMEM((levels, tile_rows, columns), F32)],
         name="weave",
         compiler_params=LIMIT,
@@ -486,16 +504,15 @@
     profiles = pl.pallas_call(
         lambda *refs: unpack_kernel(order, *refs),
         out_shape=jax.ShapeDtypeStruct((depth, tiles, slots), BF16),
-        in_specs=[VMEM],
+        in_specs=[VMEM, VMEM],
         out_specs=ANY,
         scratch_shapes=[
-            pltpu.VMEM((levels, tiles, slots), F32),
             pltpu.VMEM((levels, tiles, slots), BF16),
             pltpu.SemaphoreType.DMA((chunks,)),
         ],
         name="unpack",
         compiler_params=LIMIT,
-    )(resident(gathered))
+    )(resident(gathered), resident(swap))
     return (perturbation, jnp.transpose(profiles, (1, 0, 2))[None])
 
 

time: 32.7 us -> 32.6 us (level)
  no operation moved by 1% of the time
where the time goes in v7:
time: 32.6 us; the launch traced here: 32.2 us
  starting transfers between devices  12.9 us (40%)
  Pallas kernels  11.6 us (36%)
  waiting for transfers between devices  7.04 us (22%)
  between operations  0.65 us (2%)
    all_to_all x1, starting transfers between devices, body(): received = lax.all_to_all(packed, **exchange)  7.44 us
    all_to_all x1, waiting for transfers between devices, body(): gathered = lax.all_to_all(answers, **exchange)  6.34 us
    all_to_all x1, starting transfers between devices, body(): gathered = lax.all_to_all(answers, **exchange)  5.47 us
    pallas_call x1, Pallas kernels, body(): pl.pallas_call(lambda *refs: field_kernel(tiles, *refs), out_shape=(pltpu...  4.82 us
    pallas_call x1, Pallas kernels, body(): pl.pallas_call(lambda *refs: noise_kernel(total_rows, tile_rows, columns,...  2.96 us
    pallas_call x1, Pallas kernels, body(): pl.pallas_call(pack_kernel, out_shape=(jax.ShapeDtypeStruct((tiles, parts...  1.71 us
    pallas_call x1, Pallas kernels, body(): pl.pallas_call(weave_kernel, out_shape=(jax.ShapeDtypeStruct((depth, tile...  1.13 us
    pallas_call x1, Pallas kernels, body(): pl.pallas_call(lambda *refs: unpack_kernel(order, *refs), out_shape=jax.S...  1.01 us
  transfers between devices with their start and end apart: 2, of which 2 were waited for; matrix products, arithmetic and copies ran while one was open for 0% of the time, Pallas kernels for 13%

profile of v7, /device:TPU:1, one launch (start us, length us, event | category | flops | bytes accessed | tf_op | source)
XLA Modules:
  0.0 32.2 jit_solution(14256441999701450567)
XLA Ops:
  0.6 1.7 %pack.1 = (bf16[16,24,128]{2,1,0:T(8,128)(2,1)}, f32[8,256]{1,0:T(8,128)}, f32[8,256]{1,0:T(8,128)}) custom-call(f32[8,256]{1,0:T(8,128)} %diff_ref.1, s32[8,256]{1,0:T(8,128)} %wet_ref.1, f32[8,256]{1,0:T(8,128)} %norm_ref.1, s32[16,128]{1,0:T(8,128)} %bitcast.7, f32[16,2,128]{2,1,0:T(2,128)} %bitcast.6, s32[1,16]{1,0:T(1,128)} %count_ref.1), custom_call_target="tpu_custom_call" | custom-call | tf_op jit(solution)/shard_map/pack/pallas_call | solution.py:431
  2.3 7.4 %all-to-all-start = ((bf16[16,24,128]{2,1,0:T(8,128)(2,1)}), bf16[16,24,128]{2,1,0:T(8,128)(2,1)S(1)}, u32[]{:S(2)}, u32[]{:S(2)}) async-start(bf16[16,24,128]{2,1,0:T(8,128)(2,1)} %get-tuple-element.18), calls=%async_computation | async-start | bytes 196608 | tf_op jit(solution)/shard_map/all_to_all | solution.py:446
  9.8 3.0 %noise.1 = (f32[100,40,128]{2,1,0:T(8,128)S(1)}, f32[48,40,128]{2,1,0:T(8,128)S(1)}, f32[8,256]{1,0:T(8,128)S(1)}, f32[8,256]{1,0:T(8,128)S(1)}, bf16[80,240]{1,0:T(8,128)(2,1)S(1)}) custom-call(s32[2]{0:T(128)} %refs_0_.1, f32[8,256]{1,0:T(8,128)} %get-tuple-element.14.refs_1_, f32[8,256]{1,0:T(8,128)} %get-tuple-element.15.refs_2_, f32[75,75]{1,0:T(8,128)} %refs_3_.1), custom_call_target="tpu_custom_call" | custom-call | tf_op jit(solution)/shard_map/noise/pallas_call | solution.py:450
  12.7 0.7 %all-to-all-done.refs_2_ = bf16[16,24,128]{2,1,0:T(8,128)(2,1)S(1)} async-done(((bf16[16,24,128]{2,1,0:T(8,128)(2,1)}), bf16[16,24,128]{2,1,0:T(8,128)(2,1)S(1)}, u32[]{:S(2)}, u32[]{:S(2)}) %all-to-all-start) | async-done | bytes 98336 | tf_op jit(solution)/shard_map/all_to_all | solution.py:446
  13.4 4.8 %field.1 = (bf16[16,19,4,128]{3,2,1,0:T(4,128)(2,1)}, bf16[720,256]{1,0:T(8,128)(2,1)S(1)}) custom-call(f32[100,40,128]{2,1,0:T(8,128)S(1)} %get-tuple-element.16.refs_0_, f32[48,40,128]{2,1,0:T(8,128)S(1)} %get-tuple-element.17.refs_1_, bf16[16,24,128]{2,1,0:T(8,128)(2,1)S(1)} %all-to-all-done.refs_2_, f32[8,256]{1,0:T(8,128)S(1)} %get-tuple-element.19.refs_3_, ...), custom_call_target="tpu_custom_call" | custom-call | tf_op jit(solution)/shard_map/field/pallas_call | solution.py:467
  18.3 5.5 %all-to-all-start.1 = ((bf16[16,19,4,128]{3,2,1,0:T(4,128)(2,1)}), bf16[16,19,4,128]{3,2,1,0:T(4,128)(2,1)S(1)}, u32[]{:S(2)}, u32[]{:S(2)}) async-start(bf16[16,19,4,128]{3,2,1,0:T(4,128)(2,1)} %get-tuple-element.24), calls=%async_computation.1 | async-start | bytes 622592 | tf_op jit(solution)/shard_map/all_to_all | solution.py:490
  23.7 1.1 %weave.1 = (bf16[75,8,256]{2,1,0:T(8,128)(2,1)}, bf16[256,256]{1,0:T(8,128)(2,1)S(1)}) custom-call(bf16[720,256]{1,0:T(8,128)(2,1)S(1)} %get-tuple-element.22.field_ref), custom_call_target="tpu_custom_call" | custom-call | tf_op jit(solution)/shard_map/weave/pallas_call | solution.py:491
  24.9 6.3 %all-to-all-done.1.refs_0_ = bf16[16,19,4,128]{3,2,1,0:T(4,128)(2,1)S(1)} async-done(((bf16[16,19,4,128]{3,2,1,0:T(4,128)(2,1)}), bf16[16,19,4,128]{3,2,1,0:T(4,128)(2,1)S(1)}, u32[]{:S(2)}, u32[]{:S(2)}) %all-to-all-start.1) | async-done | bytes 311328 | tf_op jit(solution)/shard_map/all_to_all | solution.py:490
  31.2 1.0 %unpack.1 = bf16[75,16,128]{2,1,0:T(8,128)(2,1)} custom-call(bf16[16,19,4,128]{3,2,1,0:T(4,128)(2,1)S(1)} %all-to-all-done.1.refs_0_, bf16[256,256]{1,0:T(8,128)(2,1)S(1)} %get-tuple-element.25.refs_1_), custom_call_target="tpu_custom_call" | custom-call | tf_op jit(solution)/shard_map/unpack/pallas_call | solution.py:504
Async XLA Ops:
  2.3 11.1 %all-to-all-start = ((bf16[16,24,128]{2,1,0:T(8,128)(2,1)}), bf16[16,24,128]{2,1,0:T(8,128)(2,1)S(1)}, u32[]{:S(2)}, u32[]{:S(2)}) async-start(bf16[16,24,128]{2,1,0:T(8,128)(2,1)} %get-tuple-element.18), calls=%async_computation | async-start | bytes 196608 | tf_op jit(solution)/shard_map/all_to_all | solution.py:446
  18.3 12.9 %all-to-all-start.1 = ((bf16[16,19,4,128]{3,2,1,0:T(4,128)(2,1)}), bf16[16,19,4,128]{3,2,1,0:T(4,128)(2,1)S(1)}, u32[]{:S(2)}, u32[]{:S(2)}) async-start(bf16[16,19,4,128]{3,2,1,0:T(4,128)(2,1)} %get-tuple-element.24), calls=%async_computation.1 | async-start | bytes 622592 | tf_op jit(solution)/shard_map/all_to_all | solution.py:490

commit v8 on v7

--- a/solution.py
+++ b/solution.py
@@ -93,7 +93,7 @@
     lane = iota((1, LANES), 1)
     for owner in range(owners):
         at = slice(owner, owner + 1)
-        live = lane < count_ref[0, owner]
+        live = lane < count_ref[:, owner : owner + 1]
         tail = jnp.concatenate(
             norms + [col[at], high_x[at], low_x[at]]
             + [jnp.where(live, row[at], -16.0), high_y[at], low_y[at]],
@@ -435,7 +435,7 @@
             square,
             square,
         ),
-        in_specs=[VMEM] * 5 + [SMEM],
+        in_specs=[VMEM] * 6,
         out_specs=(VMEM,) * 3,
         name="pack",
     )(diffusivity, wet_mask, norm_scale, obs_cell[0], obs_frac[0], obs_count)

time: 32.6 us -> 32.6 us (level)
  no operation moved by 1% of the time
where the time goes in v8:
time: 32.6 us; the launch traced here: 32.2 us
  starting transfers between devices  12.9 us (40%)
  Pallas kernels  11.6 us (36%)
  waiting for transfers between devices  7.04 us (22%)
  between operations  0.65 us (2%)
    all_to_all x1, starting transfers between devices, body(): received = lax.all_to_all(packed, **exchange)  7.44 us
    all_to_all x1, waiting for transfers between devices, body(): gathered = lax.all_to_all(answers, **exchange)  6.34 us
    all_to_all x1, starting transfers between devices, body(): gathered = lax.all_to_all(answers, **exchange)  5.47 us
    pallas_call x1, Pallas kernels, body(): pl.pallas_call(lambda *refs: field_kernel(tiles, *refs), out_shape=(pltpu...  4.82 us
    pallas_call x1, Pallas kernels, body(): pl.pallas_call(lambda *refs: noise_kernel(total_rows, tile_rows, columns,...  2.96 us
    pallas_call x1, Pallas kernels, body(): pl.pallas_call(pack_kernel, out_shape=(jax.ShapeDtypeStruct((tiles, parts...  1.69 us
    pallas_call x1, Pallas kernels, body(): pl.pallas_call(weave_kernel, out_shape=(jax.ShapeDtypeStruct((depth, tile...  1.13 us
    pallas_call x1, Pallas kernels, body(): pl.pallas_call(lambda *refs: unpack_kernel(order, *refs), out_shape=jax.S...  1.01 us
  transfers between devices with their start and end apart: 2, of which 2 were waited for; matrix products, arithmetic and copies ran while one was open for 0% of the time, Pallas kernels for 13%

profile of v8, /device:TPU:1, one launch (start us, length us, event | category | flops | bytes accessed | tf_op | source)
XLA Modules:
  0.0 32.2 jit_solution(13658174252042674122)
XLA Ops:
  0.6 1.7 %pack.1 = (bf16[16,24,128]{2,1,0:T(8,128)(2,1)}, f32[8,256]{1,0:T(8,128)}, f32[8,256]{1,0:T(8,128)}) custom-call(f32[8,256]{1,0:T(8,128)} %diff_ref.1, s32[8,256]{1,0:T(8,128)} %wet_ref.1, f32[8,256]{1,0:T(8,128)} %norm_ref.1, s32[16,128]{1,0:T(8,128)} %bitcast.7, f32[16,2,128]{2,1,0:T(2,128)} %bitcast.6, s32[1,16]{1,0:T(1,128)} %count_ref.1), custom_call_target="tpu_custom_call" | custom-call | tf_op jit(solution)/shard_map/pack/pallas_call | solution.py:431
  2.3 7.4 %all-to-all-start = ((bf16[16,24,128]{2,1,0:T(8,128)(2,1)}), bf16[16,24,128]{2,1,0:T(8,128)(2,1)S(1)}, u32[]{:S(2)}, u32[]{:S(2)}) async-start(bf16[16,24,128]{2,1,0:T(8,128)(2,1)} %get-tuple-element.18), calls=%async_computation | async-start | bytes 196608 | tf_op jit(solution)/shard_map/all_to_all | solution.py:446
  9.8 3.0 %noise.1 = (f32[100,40,128]{2,1,0:T(8,128)S(1)}, f32[48,40,128]{2,1,0:T(8,128)S(1)}, f32[8,256]{1,0:T(8,128)S(1)}, f32[8,256]{1,0:T(8,128)S(1)}, bf16[80,240]{1,0:T(8,128)(2,1)S(1)}) custom-call(s32[2]{0:T(128)} %refs_0_.1, f32[8,256]{1,0:T(8,128)} %get-tuple-element.14.refs_1_, f32[8,256]{1,0:T(8,128)} %get-tuple-element.15.refs_2_, f32[75,75]{1,0:T(8,128)} %refs_3_.1), custom_call_target="tpu_custom_call" | custom-call | tf_op jit(solution)/shard_map/noise/pallas_call | solution.py:450
  12.7 0.7 %all-to-all-done.refs_2_ = bf16[16,24,128]{2,1,0:T(8,128)(2,1)S(1)} async-done(((bf16[16,24,128]{2,1,0:T(8,128)(2,1)}), bf16[16,24,128]{2,1,0:T(8,128)(2,1)S(1)}, u32[]{:S(2)}, u32[]{:S(2)}) %all-to-all-start) | async-done | bytes 98336 | tf_op jit(solution)/shard_map/all_to_all | solution.py:446
  13.4 4.8 %field.1 = (bf16[16,19,4,128]{3,2,1,0:T(4,128)(2,1)}, bf16[720,256]{1,0:T(8,128)(2,1)S(1)}) custom-call(f32[100,40,128]{2,1,0:T(8,128)S(1)} %get-tuple-element.16.refs_0_, f32[48,40,128]{2,1,0:T(8,128)S(1)} %get-tuple-element.17.refs_1_, bf16[16,24,128]{2,1,0:T(8,128)(2,1)S(1)} %all-to-all-done.refs_2_, f32[8,256]{1,0:T(8,128)S(1)} %get-tuple-element.19.refs_3_, ...), custom_call_target="tpu_custom_call" | custom-call | tf_op jit(solution)/shard_map/field/pallas_call | solution.py:467
  18.3 5.5 %all-to-all-start.1 = ((bf16[16,19,4,128]{3,2,1,0:T(4,128)(2,1)}), bf16[16,19,4,128]{3,2,1,0:T(4,128)(2,1)S(1)}, u32[]{:S(2)}, u32[]{:S(2)}) async-start(bf16[16,19,4,128]{3,2,1,0:T(4,128)(2,1)} %get-tuple-element.24), calls=%async_computation.1 | async-start | bytes 622592 | tf_op jit(solution)/shard_map/all_to_all | solution.py:490
  23.7 1.1 %weave.1 = (bf16[75,8,256]{2,1,0:T(8,128)(2,1)}, bf16[256,256]{1,0:T(8,128)(2,1)S(1)}) custom-call(bf16[720,256]{1,0:T(8,128)(2,1)S(1)} %get-tuple-element.22.field_ref), custom_call_target="tpu_custom_call" | custom-call | tf_op jit(solution)/shard_map/weave/pallas_call | solution.py:491
  24.9 6.3 %all-to-all-done.1.refs_0_ = bf16[16,19,4,128]{3,2,1,0:T(4,128)(2,1)S(1)} async-done(((bf16[16,19,4,128]{3,2,1,0:T(4,128)(2,1)}), bf16[16,19,4,128]{3,2,1,0:T(4,128)(2,1)S(1)}, u32[]{:S(2)}, u32[]{:S(2)}) %all-to-all-start.1) | async-done | bytes 311328 | tf_op jit(solution)/shard_map/all_to_all | solution.py:490
  31.2 1.0 %unpack.1 = bf16[75,16,128]{2,1,0:T(8,128)(2,1)} custom-call(bf16[16,19,4,128]{3,2,1,0:T(4,128)(2,1)S(1)} %all-to-all-done.1.refs_0_, bf16[256,256]{1,0:T(8,128)(2,1)S(1)} %get-tuple-element.25.refs_1_), custom_call_target="tpu_custom_call" | custom-call | tf_op jit(solution)/shard_map/unpack/pallas_call | solution.py:504
Async XLA Ops:
  2.3 11.1 %all-to-all-start = ((bf16[16,24,128]{2,1,0:T(8,128)(2,1)}), bf16[16,24,128]{2,1,0:T(8,128)(2,1)S(1)}, u32[]{:S(2)}, u32[]{:S(2)}) async-start(bf16[16,24,128]{2,1,0:T(8,128)(2,1)} %get-tuple-element.18), calls=%async_computation | async-start | bytes 196608 | tf_op jit(solution)/shard_map/all_to_all | solution.py:446
  18.3 12.9 %all-to-all-start.1 = ((bf16[16,19,4,128]{3,2,1,0:T(4,128)(2,1)}), bf16[16,19,4,128]{3,2,1,0:T(4,128)(2,1)S(1)}, u32[]{:S(2)}, u32[]{:S(2)}) async-start(bf16[16,19,4,128]{3,2,1,0:T(4,128)(2,1)} %get-tuple-element.24), calls=%async_computation.1 | async-start | bytes 622592 | tf_op jit(solution)/shard_map/all_to_all | solution.py:490
